TPU v7x, 128 devices: a whole 4x4x4 slice. The times are simulated.
128 devices in a mesh: row: 16 (over x, y_lo, core), col: 8 (over y_hi, z).
Axes of the slice: x: 4, y: 4 (y_hi: 2, y_lo: 2; y = y_hi * 2 + y_lo), z: 4, core: 2. Of those that a mesh axis runs over, the one named last changes fastest.
Arguments:
- hidden_states: bfloat16 [16384, 2048], P('row', 'col'), may hold values from -21 to 21
- lengths: int32 [32], P('row'), may hold values from 16 to 512, as said below
- qkvg_master: float32 [2048, 12288], P(('row', 'col')), may hold values from -0.125 to 0.125
- gateup_master: float32 [2, 2048, 4096], P(None, ('row', 'col')), may hold values from -0.125 to 0.125
- out_master: float32 [4096, 2048], P(None, ('row', 'col')), may hold values from -0.09375 to 0.09375
- down_master: float32 [4096, 2048], P(None, ('row', 'col')), may hold values from -0.09375 to 0.09375
Outputs:
- layer_output: bfloat16 [16384, 2048], P('row', 'col')
- qkvg_weight: bfloat16 [2048, 12288], P('row', 'col')
- gateup_weight: bfloat16 [2, 2048, 4096], P(None, 'row', 'col')
- mixing_weight: bfloat16 [4096, 2048], P('col', 'row')
- down_weight: bfloat16 [4096, 2048], P('col', 'row')
Inputs may be any that keep to these rules, and one draw needn't show every extreme that they name: `lengths`: prompt length of each request; the positions of a request from its length on are padding. Some request has length 512 in every draw.
All inputs are finite; a program needn't handle non-finite values.
Results may differ from a plain program's by a relative error of at most 0.014.
Values may be sent and summed in bfloat16 or wider, within the bound.
A program may use at most 128 MiB of HBM per device.

v0:
```python
import math

import jax
import jax.numpy as jnp
from jax import lax
from jax.sharding import PartitionSpec as P

D = 2048
HEADS = 8
KEY = 256
VAL = 512
S = 512
BLOCK = 256


epsilon = 1e-05


def rms_round(values):
    scale = lax.rsqrt(jnp.mean(values * values, axis=-1, keepdims=True) + epsilon)
    return (values * scale).astype(jnp.bfloat16)


def rotate(values, positions):
    half = values.shape[-1] // 2
    freq = jnp.power(10000.0, -2.0 * jnp.arange(half).astype(jnp.float32) / values.shape[-1])
    angle = positions.astype(jnp.float32)[:, None] * freq[None, :]
    cosine = jnp.cos(angle)[:, None, :]
    sine = jnp.sin(angle)[:, None, :]
    first = values[..., :half]
    second = values[..., half:]
    return jnp.concatenate(
        [first * cosine - second * sine, first * sine + second * cosine], axis=-1
    )


def retain(gammas, query, keyed, value):
    heads = query.shape[1]
    blocks = S // BLOCK
    offsets = jnp.arange(BLOCK)
    lag = offsets[:, None] - offsets[None, :]
    within = jnp.where(
        (lag >= 0)[None],
        jnp.power(gammas[:, None, None], jnp.maximum(lag, 0).astype(jnp.float32)[None]),
        0.0,
    )
    into = jnp.power(gammas[:, None], (offsets + 1).astype(jnp.float32)[None, :])
    leaving = jnp.power(gammas[:, None], (BLOCK - 1 - offsets).astype(jnp.float32)[None, :])
    across_blocks_sum = jnp.power(gammas, 1.0 * BLOCK)
    upper_bound = lax.Precision.HIGHEST

    def advance(carry, inputs):
        retention_state, key_sum = carry
        query_block, key_block, value_tile_rows = inputs
        scores = (
            jnp.einsum("thk,shk->hts", query_block, key_block, preferred_element_type=jnp.float32)
            * within
        )
        denom_inside = jnp.sum(scores, axis=2)
        inside = jnp.einsum(
            "hts,shv->thv",
            scores.astype(jnp.bfloat16),
            value_tile_rows,
            preferred_element_type=jnp.float32,
        )
        damped_query_rows = query_block.astype(jnp.float32) * jnp.transpose(into)[:, :, None]
        carried_state = jnp.einsum(
            "swc,wcm->swm", damped_query_rows, retention_state, precision=upper_bound
        )
        denom_carried = jnp.einsum("thk,hk->th", damped_query_rows, key_sum, precision=upper_bound)
        damped_key_rows = key_block.astype(jnp.float32) * jnp.transpose(leaving)[:, :, None]
        retention_state = across_blocks_sum[:, None, None] * retention_state + jnp.einsum(
            "wat,wag->atg",
            damped_key_rows,
            value_tile_rows.astype(jnp.float32),
            precision=upper_bound,
        )
        key_sum = across_blocks_sum[:, None] * key_sum + jnp.sum(damped_key_rows, axis=0)
        denom = jnp.transpose(denom_inside) + denom_carried
        result = (inside + carried_state) / jnp.maximum(jnp.abs(denom), 1.0)[:, :, None]
        return ((retention_state, key_sum), result)

    start = (jnp.zeros((heads, KEY, VAL), jnp.float32), jnp.zeros((heads, KEY), jnp.float32))
    sliced = (
        query.reshape(blocks, BLOCK, heads, KEY),
        keyed.reshape(blocks, BLOCK, heads, KEY),
        value.reshape(blocks, BLOCK, heads, VAL),
    )
    _, results = lax.scan(advance, start, sliced)
    return results.reshape(S, heads, VAL)


def gate_heads(retained, gate):
    centre = jnp.mean(retained, axis=-1, keepdims=True)
    centred = retained - centre
    spread = jnp.mean(centred * centred, axis=-1, keepdims=True)
    grouped = centred * lax.rsqrt(spread + epsilon)
    return (jax.nn.silu(gate.astype(jnp.float32)) * grouped).astype(jnp.bfloat16)


def shards(hidden_states, lengths, qkvg_master, gateup_master, out_master, down_master):
    tok_rows = hidden_states.shape[0]
    share_width = hidden_states.shape[1]
    requests = lengths.shape[0]
    head_count = HEADS // lax.axis_size("col")
    head_width = 2 * KEY + 2 * VAL
    in_blocks = (
        lax.all_to_all(
            qkvg_master.astype(jnp.bfloat16)[None], "col", split_axis=2, concat_axis=1, tiled=True
        ),
        lax.all_to_all(
            gateup_master.astype(jnp.bfloat16), "col", split_axis=2, concat_axis=1, tiled=True
        ),
    )
    qkvg_blocks = in_blocks[0][0]
    gateup_blocks = in_blocks[1]
    out_blocks, down_blocks = (
        lax.all_to_all(
            out_master.astype(jnp.bfloat16), "col", split_axis=0, concat_axis=1, tiled=True
        ),
        lax.all_to_all(
            down_master.astype(jnp.bfloat16), "col", split_axis=0, concat_axis=1, tiled=True
        ),
    )
    gathered = lax.all_gather(hidden_states, "col", axis=1, tiled=True)
    normed = rms_round(gathered.astype(jnp.float32))
    columns = normed
    projected = jnp.dot(
        columns,
        lax.all_gather(qkvg_blocks, "row", axis=0, tiled=True),
        preferred_element_type=jnp.float32,
    )
    projected = projected.astype(jnp.bfloat16).reshape(requests, S, head_count, head_width)
    positions = jnp.arange(S)
    query = rotate(projected[..., :KEY].astype(jnp.float32), positions).astype(jnp.bfloat16)
    keyed = (
        rotate(projected[..., KEY : 2 * KEY].astype(jnp.float32), positions)
        * (1.0 / math.sqrt(KEY))
    ).astype(jnp.bfloat16)
    value = projected[..., 2 * KEY : 2 * KEY + VAL]
    gate = projected[..., 2 * KEY + VAL :]
    head_ids = lax.axis_index("col") * head_count + jnp.arange(head_count)
    gammas = 1.0 - jnp.power(2.0, -5.0 - head_ids.astype(jnp.float32))
    retained = jax.vmap(retain, in_axes=(None, 0, 0, 0))(gammas, query, keyed, value)
    mixed = gate_heads(retained, gate).reshape(tok_rows, head_count * VAL)
    partial_mix = jnp.dot(
        mixed,
        lax.all_gather(out_blocks, "row", axis=1, tiled=True),
        preferred_element_type=jnp.float32,
    )
    residual = hidden_states.astype(jnp.float32) + lax.psum_scatter(
        partial_mix.astype(jnp.bfloat16), "col", scatter_dimension=1, tiled=True
    ).astype(jnp.float32)
    squares = lax.psum(jnp.sum(residual * residual, axis=1), "col")
    normed_share = (residual * lax.rsqrt(squares[:, None] / D + epsilon)).astype(jnp.bfloat16)
    normed_mid = lax.all_gather(normed_share, "col", axis=1, tiled=True)
    columns = normed_mid
    paired = jnp.einsum(
        "td,gdf->gtf",
        columns,
        lax.all_gather(gateup_blocks, "row", axis=1, tiled=True),
        preferred_element_type=jnp.float32,
    )
    hidden = (jax.nn.silu(paired[0]) * paired[1]).astype(jnp.bfloat16)
    partial_feed = jnp.dot(
        hidden,
        lax.all_gather(down_blocks, "row", axis=1, tiled=True),
        preferred_element_type=jnp.float32,
    )
    feed = lax.psum_scatter(
        partial_feed.astype(jnp.bfloat16), "col", scatter_dimension=1, tiled=True
    ).astype(jnp.float32)
    live = positions[None, :] < lengths[:, None]
    summed = (residual + feed).reshape(requests, S, share_width)
    layer_output = (
        jnp.where(live[:, :, None], summed, 0.0).astype(jnp.bfloat16).reshape(tok_rows, share_width)
    )
    return (layer_output, qkvg_blocks, gateup_blocks, out_blocks, down_blocks)


def solution(mesh):
    return jax.shard_map(
        shards,
        mesh=mesh,
        in_specs=(
            P("row", "col"),
            P("row"),
            P(("row", "col"), None),
            P(None, ("row", "col"), None),
            P(None, ("row", "col")),
            P(None, ("row", "col")),
        ),
        out_specs=(
            P("row", "col"),
            P("row", "col"),
            P(None, "row", "col"),
            P("col", "row"),
            P("col", "row"),
        ),
        check_vma=False,
    )
```

profile of v0, /device:TPU:1, one launch (start us, length us, event | category | flops | bytes accessed | tf_op | source)
XLA Modules:
  0.0 546.0 jit_solution(4470054809173031747)
XLA Ops:
  9.1 9.8 %copy.81 = bf16[1,16,12288]{1,0,2:T(2,128)(2,1)} copy(bf16[1,16,12288]{2,1,0:T(8,128)(2,1)S(1)} %convert_bitcast_fusion) | data formatting | bytes 786432 | tf_op jit(solution)/shard_map/broadcast_in_dim | solution.py:109
  19.4 67.0 %reduce.7 = bf16[12288,16]{1,0:T(8,128)(2,1)S(1)} reduce(bf16[12288,1,16]{2,1,0:T(2,128)(2,1)} %bitcast.202, bf16[]{:T(256)} %broadcast.312), dimensions={1}, to_apply=%bitcast.147.reduce_sub_computation | reduce | bytes 786434
  86.4 3.3 reshape.460
  89.7 16.9 %all_to_all.71 = bf16[8,2,12288]{2,1,0:T(2,128)(2,1)S(1)} all-to-all(bf16[8,2,12288]{2,1,0:T(2,128)(2,1)S(1)} %reshape.460), channel_id=1, replica_groups=mesh['row'=16,'col'=8] {'col'}, dimensions={0} | all-to-all | bytes 786432 | tf_op jit(solution)/shard_map/all_to_all | solution.py:108
  106.6 6.2 %reshape.461 = bf16[12288,1,16]{2,1,0:T(2,128)(2,1)} reshape(bf16[8,2,12288]{2,1,0:T(2,128)(2,1)S(1)} %all_to_all.71) | data formatting | bytes 786432
  112.9 11.4 %copy.82 = bf16[1,16,12288]{2,1,0:T(8,128)(2,1)S(1)} copy(bf16[1,16,12288]{1,0,2:T(2,128)(2,1)} %bitcast.203) | data formatting | bytes 786432 | tf_op jit(solution)/shard_map/all_to_all | solution.py:108
  126.0 3.5 all-to-all-start.1
  130.7 5.8 %all-to-all-done.1 = bf16[8,512,16]{1,2,0:T(8,128)(2,1)S(1)} async-done(((bf16[8,512,16]{1,2,0:T(8,128)(2,1)}), bf16[8,512,16]{1,2,0:T(8,128)(2,1)S(1)}, u32[]{:S(2)}, u32[]{:S(2)}) %all-to-all-start.1) | async-done | bytes 131104 | tf_op jit(solution)/shard_map/all_to_all | solution.py:118
  137.4 3.2 fusion.45
  140.6 26.6 %all-gather.9.cloned.1.call-done = bf16[2048,1536]{1,0:T(8,128)(2,1)} async-done(((bf16[128,1536]{1,0:T(8,128)(2,1)}), bf16[2048,1536]{1,0:T(8,128)(2,1)}) %all-gather.9.cloned.1.call-update) | async-done | bytes 6291472 | tf_op jit(solution)/shard_map/all_gather | solution.py:130
  167.2 10.5 %fusion.52 = bf16[1024,1536]{1,0:T(8,128)(2,1)S(1)} fusion(bf16[2048,1536]{1,0:T(8,128)(2,1)} %all-gather.9.cloned.1.call-done, bf16[1024,2048]{1,0:T(8,128)(2,1)} %all-gather.7.cloned.1.call-done, f32[1024]{0:T(1024)S(1)} %add_rsqrt_fusion.1), kind=kOutput, calls=%fused_computation.65 | convolution fusion | flops 6450315264 | bytes 13635584 | tf_op jit(solution)/shard_map/dot_general | solution.py:128
  179.8 18.9 %while.17 = (s32[]{:T(128)}, f32[2,1,256,512]{3,2,0,1:T(8,128)S(1)}, f32[2,1,256]{2,1,0:T(1,128)S(1)}, f32[2,2,256,1,512]{4,2,0,1,3:T(8,128)}, f32[1]{0:T(128)},...) while((s32[]{:T(128)}, ...), condition=%wide.region_4.5_spmd.clone.clone.clone, body=%wide.region_1.4_spmd.clone.clone.clone.sunk | while | flops 1816989184 | bytes 22576332 | solution.py:89
  181.1 2.0 convolution_bitcast_fusion.3
  187.1 2.0 fusion.98
  196.5 2.0 fusion.98
  201.4 2.1 fusion.67
  204.4 5.9 %convolution_convert_fusion.1 = bf16[1024,2048]{1,0:T(8,128)(2,1)} fusion(bf16[1024,512]{1,0:T(8,128)(2,1)S(1)} %bitcast.224, bf16[512,2048]{0,1:T(8,128)(2,1)} %all-gather.11.cloned.1.call-done), kind=kOutput, calls=%fused_computation.67 | convolution fusion | flops 2149580800 | bytes 7340032 | tf_op jit(solution)/shard_map/dot_general | solution.py:146
  211.4 2.7 copy.89
  214.1 2.2 reshape.458
  216.3 16.4 %all_to_all.72 = bf16[8,2,8192]{2,1,0:T(2,128)(2,1)S(1)} all-to-all(bf16[8,2,8192]{2,1,0:T(2,128)(2,1)S(1)} %reshape.458), channel_id=1, replica_groups=mesh['row'=16,'col'=8] {'col'}, dimensions={0} | all-to-all | bytes 524288 | tf_op jit(solution)/shard_map/all_to_all | solution.py:111
  234.1 3.3 copy.90
  237.4 58.7 %reduce-scatter.3.cloned.1.call-done = bf16[1024,256]{1,0:T(8,128)(2,1)} async-done(((bf16[1024,2048]{1,0:T(8,128)(2,1)}), bf16[1024,256]{1,0:T(8,128)(2,1)}) %reduce-scatter.3.cloned.1.call-update) | async-done | bytes 524304 | tf_op jit(solution)/shard_map/reduce_scatter | solution.py:151
  297.5 17.0 %psum.7 = f32[1024]{0:T(1024)S(1)} all-reduce(f32[1024]{0:T(1024)S(1)} %multiply_reduce_fusion), channel_id=1, replica_groups=mesh['row'=16,'col'=8] {'col'}, use_global_device_ids=true, to_apply=%region_9.10 | all-reduce | flops 1024 | bytes 8192 | tf_op jit(solution)/shard_map/psum | solution.py:154
  314.5 2.1 multiply_convert_fusion
  316.7 11.3 %all_to_all.73 = bf16[8,512,16]{1,2,0:T(8,128)(2,1)} all-to-all(bf16[8,512,16]{1,2,0:T(8,128)(2,1)S(1)} %bitcast.227), channel_id=1, replica_groups=mesh['row'=16,'col'=8] {'col'}, dimensions={0} | all-to-all | bytes 262144 | tf_op jit(solution)/shard_map/all_to_all | solution.py:121
  328.1 8.4 %all-gather.15.cloned.1.call-done = bf16[2,2048,512]{2,1,0:T(8,128)(2,1)} async-done(((bf16[2,128,512]{2,1,0:T(8,128)(2,1)}), bf16[2,2048,512]{2,1,0:T(8,128)(2,1)}) %all-gather.15.cloned.1.call-update) | async-done | bytes 4194320 | tf_op jit(solution)/shard_map/all_gather | solution.py:161
  336.5 75.5 %all-gather.13.cloned.1.call-done = bf16[1024,2048]{1,0:T(8,128)(2,1)} async-done(((bf16[1024,256]{1,0:T(8,128)(2,1)}), bf16[1024,2048]{1,0:T(8,128)(2,1)}) %all-gather.13.cloned.1.call-update) | async-done | bytes 4194320 | tf_op jit(solution)/shard_map/all_gather | solution.py:156
  412.0 9.9 %fusion.55 = f32[2,1024,512]{2,1,0:T(8,128)} fusion(bf16[2,2048,512]{2,1,0:T(8,128)(2,1)} %all-gather.15.cloned.1.call-done, bf16[1024,2048]{1,0:T(8,128)(2,1)} %all-gather.13.cloned.1.call-done), kind=kOutput, calls=%fused_computation.70 | convolution fusion | flops 4294967296 | bytes 12582912 | tf_op jit(solution)/shard_map/td,gdf->gtf/dot_general | solution.py:158
  421.9 24.5 %all-gather.17.cloned.1.call-done = bf16[512,2048]{0,1:T(8,128)(2,1)} async-done(((bf16[512,128]{0,1:T(8,128)(2,1)}), bf16[512,2048]{0,1:T(8,128)(2,1)}) %all-gather.17.cloned.1.call-update) | async-done | bytes 2097168 | tf_op jit(solution)/shard_map/all_gather | solution.py:167
  446.4 7.2 %convolution_convert_fusion = bf16[1024,2048]{1,0:T(8,128)(2,1)} fusion(bf16[512,2048]{0,1:T(8,128)(2,1)} %all-gather.17.cloned.1.call-done, f32[2,1024,512]{2,1,0:T(8,128)} %fusion.55), kind=kOutput, calls=%fused_computation.66 | convolution fusion | flops 2152726528 | bytes 10485760 | tf_op jit(solution)/shard_map/dot_general | solution.py:165
  456.1 81.1 %reduce-scatter.5.cloned.1.call-done = bf16[1024,256]{1,0:T(8,128)(2,1)} async-done(((bf16[1024,2048]{1,0:T(8,128)(2,1)}), bf16[1024,256]{1,0:T(8,128)(2,1)}) %reduce-scatter.5.cloned.1.call-update) | async-done | bytes 524304 | tf_op jit(solution)/shard_map/reduce_scatter | solution.py:170
  537.1 2.1 select_convert_fusion
  (104 shorter events, 30.8 us)
Async XLA Ops:
  7.2 130.2 %all-gather.7.cloned.1.call-start = ((), (), s32[]{:S(2)}) async-start(), calls=%async_computation.6 | async-start | bytes 4718592 | tf_op jit(solution)/shard_map/all_gather | solution.py:125
  7.9 159.3 %all-gather.9.cloned.1.call-start = ((), (), s32[]{:S(2)}) async-start(), calls=%async_computation.7 | async-start | bytes 6684672 | tf_op jit(solution)/shard_map/all_gather | solution.py:130
  124.3 1.1 copy-start.10
  126.0 10.4 %all-to-all-start.1 = ((bf16[8,512,16]{1,2,0:T(8,128)(2,1)}), bf16[8,512,16]{1,2,0:T(8,128)(2,1)S(1)}, u32[]{:S(2)}, u32[]{:S(2)}) async-start(bf16[8,512,16]{1,2,0:T(8,128)(2,1)} %bitcast.160), calls=%async_computation.1 | async-start | bytes 262144 | tf_op jit(solution)/shard_map/all_to_all | solution.py:118
  129.5 74.9 %all-gather.11.cloned.1.call-start = ((), (), s32[]{:S(2)}) async-start(), calls=%async_computation.8 | async-start | bytes 2228224 | tf_op jit(solution)/shard_map/all_gather | solution.py:148
  136.5 0.7 copy-start.6
  137.2 159.0 %reduce-scatter.3.cloned.1.call-start = ((), (), s32[]{:S(2)}) async-start(), calls=%async_computation.9 | async-start | bytes 4718592 | tf_op jit(solution)/shard_map/reduce_scatter | solution.py:151
  177.7 1.7 copy-start.5
  179.8 3.3 copy-start.1
  187.1 2.2 copy-start.2
  189.3 3.3 copy-start.1
  196.5 2.1 copy-start.2
  198.7 2.2 copy-start
  210.3 1.0 copy-start.9
  210.3 126.1 %all-gather.15.cloned.1.call-start = ((), (), s32[]{:S(2)}) async-start(), calls=%async_computation.11 | async-start | bytes 4456448 | tf_op jit(solution)/shard_map/all_gather | solution.py:161
  232.7 63.5 %copy-start.3 = (bf16[1024,256]{1,0:T(8,128)(2,1)S(1)}, bf16[1024,256]{1,0:T(8,128)(2,1)}, u32[]{:S(2)}) copy-start(bf16[1024,256]{1,0:T(8,128)(2,1)} %param.8) | copy-start | bytes 1572868
  237.4 79.3 %copy-start.11 = (f32[4096,16]{0,1:T(8,128)S(1)}, f32[4096,16]{0,1:T(8,128)}, u32[]{:S(2)}) copy-start(f32[4096,16]{0,1:T(8,128)} %param.13) | copy-start | bytes 786436
  237.4 174.6 %all-gather.13.cloned.1.call-start = ((), (), s32[]{:S(2)}) async-start(), calls=%async_computation.10 | async-start | bytes 4718592 | tf_op jit(solution)/shard_map/all_gather | solution.py:156
  316.6 129.8 %all-gather.17.cloned.1.call-start = ((), (), s32[]{:S(2)}) async-start(), calls=%async_computation.12 | async-start | bytes 2228224 | tf_op jit(solution)/shard_map/all_gather | solution.py:167
  328.0 209.1 %reduce-scatter.5.cloned.1.call-start = ((), (), s32[]{:S(2)}) async-start(), calls=%async_computation.13 | async-start | bytes 4718592 | tf_op jit(solution)/shard_map/reduce_scatter | solution.py:170
  453.6 0.7 copy-start.12
  453.6 0.9 copy-start.7
  453.6 1.7 copy-start.8
  453.6 83.5 %copy-start.4 = (bf16[1024,256]{1,0:T(8,128)(2,1)S(1)}, bf16[1024,256]{1,0:T(8,128)(2,1)}, u32[]{:S(2)}) copy-start(bf16[1024,256]{1,0:T(8,128)(2,1)} %reduce-scatter.3.cloned.1.call-done) | copy-start | bytes 1572868
Sparse Core Ops, SparseCore 0:
  10.2 76.6 all-gather.6
  125.5 41.7 all-gather.8
  169.5 34.8 all-gather.10
  210.5 85.6 reduce-scatter.2
  298.3 38.0 all-gather.14
  339.3 72.6 all-gather.12
  413.8 32.5 all-gather.16
  453.8 83.3 reduce-scatter.4
where the time goes:
time: 547 us; the launch traced here: 546 us
  waiting for transfers between devices  282 us (52%)
  other arithmetic  84 us (15%)
  blocking collectives  61.6 us (11%)
  local copies, waits for them, and re-layouts  53.3 us (10%)
  matrix products  46 us (8%)
  between operations  14.5 us (3%)
    reduce_scatter x1, waiting for transfers between devices, shards(): lax.psum_scatter(partial_feed.astype(jnp.bfloat16), 'col', scatter_dimens...  81.1 us
    all_gather x1, waiting for transfers between devices, shards(): normed_mid = lax.all_gather(normed_share, 'col', axis=1, tiled=True)  75.5 us
    unnamed x5, other arithmetic  67 us
    reduce_scatter x1, waiting for transfers between devices, shards(): lax.psum_scatter(partial_mix.astype(jnp.bfloat16), 'col', scatter_dimensi...  58.7 us
    all_gather x1, waiting for transfers between devices, shards(): lax.all_gather(qkvg_blocks, 'row', axis=0, tiled=True)  26.6 us
    all_gather x1, waiting for transfers between devices, shards(): lax.all_gather(down_blocks, 'row', axis=1, tiled=True)  24.5 us
    unnamed x32, local copies, waits for them, and re-layouts  19.1 us
    psum x1, blocking collectives, shards(): squares = lax.psum(jnp.sum(residual * residual, axis=1), 'col')  17 us
  transfers between devices with their start and end apart: 9, of which 8 were waited for; matrix products, arithmetic and copies ran while one was open for 30% of the time, Pallas kernels for 0%

commit v1 on v0

v1 whole, which is shorter than its diff:
```python
import math

import jax
import jax.numpy as jnp
import numpy as np
from jax import lax
from jax.experimental import pallas as pl
from jax.experimental.pallas import tpu as pltpu
from jax.sharding import PartitionSpec as P

D = 2048
HEADS = 8
KEY = 256
VAL = 512
S = 512
BLOCK = 256
FF = 4096
WIDE = 2 * KEY + 2 * VAL
TOK = 1024
FEAT = 256
REQS = 2
EPS = 1e-05
MESH = pl.DeviceIdType.MESH
BF = jnp.bfloat16
F32 = jnp.float32
NT = (((1,), (1,)), ((), ()))


def tables():
    half = KEY // 2
    freq = np.power(np.float32(10000.0), (-2.0 * np.arange(half) / KEY).astype(np.float32))
    angle = np.arange(S, dtype=np.float32)[:, None] * freq.astype(np.float32)[None, :]
    return np.cos(angle).astype(np.float32), np.sin(angle).astype(np.float32)


def kernel(
    hid, qm, gm, om, dm, cosr, sinr,
    y, oq, of, oo,
    sbq, sbo, sbf, srvq, srvo, srvf,
    xg, xm, gq, go, gf, acc, scl, near, far, qs, ks, mixed, hidden,
    part, pairs, relay, final, resid, outb, swapb,
    send_sem, sem_a2a, sem_own, sem_w, sem_x, sem_core, sem_rel, sem_fin, sem_swap, loc_sem,
):
    row = lax.axis_index("row")
    col = lax.axis_index("col")
    x = lax.div(row, 4)
    u = lax.rem(lax.div(row, 2), 2)
    c = lax.rem(row, 2)
    h = lax.div(col, 4)
    z = lax.rem(col, 4)
    v = 1 - u
    xp, xn, xo = lax.rem(x + 1, 4), lax.rem(x + 3, 4), lax.rem(x + 2, 4)
    zp, zn, zo = lax.rem(z + 1, 4), lax.rem(z + 3, 4), lax.rem(z + 2, 4)
    source = c == h

    def device(xx, uu, cc, hh, zz):
        return (xx * 4 + uu * 2 + cc, hh * 4 + zz)

    to_core = device(x, u, 1 - c, h, z)
    to_swap = device(x, u, h, c, z)
    to_xp, to_xn = device(xp, u, c, h, z), device(xn, u, c, h, z)
    to_zp, to_zn = device(x, u, c, h, zp), device(x, u, c, h, zn)
    to_ya, to_yb = device(x, v, c, h, z), device(x, v, c, 1 - h, z)

    pending = []
    count = [0]

    def post(build, target, when=None):
        index = count[0]
        count[0] += 1

        def copy():
            src, dst, recv = build()
            return pltpu.make_async_remote_copy(
                src_ref=src,
                dst_ref=dst,
                send_sem=send_sem.at[index],
                recv_sem=recv,
                device_id=target,
                device_id_type=MESH,
            )

        copy().start()
        pending.append((when, copy))

    def arrived(dst, recv):
        pltpu.make_async_remote_copy(
            src_ref=dst,
            dst_ref=dst,
            send_sem=send_sem.at[0],
            recv_sem=recv,
            device_id=to_core,
            device_id_type=MESH,
        ).wait_recv()

    barrier = pltpu.get_barrier_semaphore()
    peers = [(row, lax.rem(col + i, 8)) for i in range(1, 8)]
    swap_peer = device(x, u, 1 - c, 1 - h, z)
    greet = peers + [to_core, swap_peer, to_xp, to_xn, to_ya, to_yb]
    for peer in greet:
        pl.semaphore_signal(barrier, inc=1, device_id=peer, device_id_type=MESH)
    for i in range(8):
        sbq[i] = qm[:, i * WIDE : (i + 1) * WIDE].astype(BF)
    pl.semaphore_wait(barrier, len(greet))

    def exchange(buf, serve, group):
        rows = pl.ds(pl.multiple_of(col * 16, 16), 16)
        for i in range(1, 8):
            other = lax.rem(col + i, 8)
            post(
                lambda i=i, other=other: (
                    buf.at[other], serve.at[rows, :], sem_a2a.at[group * 8 + i]
                ),
                (row, other),
            )
        serve[rows, :] = buf[col]

    def exchanged(serve, group):
        for i in range(1, 8):
            sender = lax.rem(col + 8 - i, 8)
            rows = pl.ds(pl.multiple_of(sender * 16, 16), 16)
            arrived(serve.at[rows, :], sem_a2a.at[group * 8 + i])

    exchange(sbq, srvq, 0)

    def lanes(slot):
        return pl.ds(pl.multiple_of(slot * FEAT, FEAT), FEAT)

    mine = c * 4 + z

    def start_swap():
        @pl.when(jnp.logical_not(source))
        def _():
            post(lambda: (hid, xg.at[:, lanes(col)], sem_swap.at[0]), to_swap, "receiver")

        @pl.when(source)
        def _():
            xg[:, lanes(col)] = hid[...]

    start_swap()

    for i in range(8):
        sbo[i] = om[:, i * VAL : (i + 1) * VAL].astype(BF)
        sbf[i, :, 0:512] = gm[0, :, i * 512 : (i + 1) * 512].astype(BF)
        sbf[i, :, 512:1024] = gm[1, :, i * 512 : (i + 1) * 512].astype(BF)
        sbf[i, :, 1024:1536] = dm[:, i * 512 : (i + 1) * 512].astype(BF)
    exchange(sbo, srvo, 1)
    exchange(sbf, srvf, 2)

    head = c * 4 + z
    rate = jnp.float32(0.0)
    for i in range(HEADS):
        rate = jnp.where(head == i, jnp.float32(math.log1p(-(2.0 ** (-5 - i)))), rate)
    lag = lax.broadcasted_iota(jnp.int32, (BLOCK, BLOCK), 0) - lax.broadcasted_iota(
        jnp.int32, (BLOCK, BLOCK), 1
    )
    near[...] = jnp.where(lag >= 0, jnp.exp(jnp.maximum(lag, 0).astype(F32) * rate), 0.0)
    far[...] = jnp.exp((lag + BLOCK).astype(F32) * rate)

    def act_ref(buf, rows, slot):
        return buf.at[rows, lanes(slot)]

    def act_post(buf, rows, slot, recv, to):
        post(lambda: (act_ref(buf, rows, slot), act_ref(buf, rows, slot), recv), to)

    def gather_start(buf, first, size, bank):
        rows = pl.ds(first, size)
        for to in (to_zp, to_zn, to_core):
            act_post(buf, rows, mine, sem_x.at[bank * 16 + mine * 2], to)

    def gather_near(buf, first, size, bank):
        rows = pl.ds(first, size)
        half = size // 2
        for zz, start, to, part_id in ((zn, first, to_zp, 0), (zp, first + half, to_zn, 1)):
            slot = c * 4 + zz
            here = act_ref(buf, rows, slot)
            arrived(here, sem_x.at[bank * 16 + slot * 2])
            act_post(buf, pl.ds(start, half), slot, sem_x.at[bank * 16 + slot * 2 + part_id], to)
            act_post(buf, rows, slot, sem_x.at[bank * 16 + slot * 2], to_core)

    def gather_far(buf, first, size, bank):
        rows = pl.ds(first, size)
        half = size // 2
        slot = c * 4 + zo
        for part_id in range(2):
            arrived(
                act_ref(buf, pl.ds(first + part_id * half, half), slot),
                sem_x.at[bank * 16 + slot * 2 + part_id],
            )
        act_post(buf, rows, slot, sem_x.at[bank * 16 + slot * 2], to_core)

    def gather_core(buf, first, size, bank):
        rows = pl.ds(first, size)
        for zz in (z, zn, zp, zo):
            slot = (1 - c) * 4 + zz
            arrived(act_ref(buf, rows, slot), sem_x.at[bank * 16 + slot * 2])

    def weights(buf, serve, bank):
        xs = (x, xn, xp, xo)

        def block(xx, uu, cc, half=None):
            start = (xx * 4 + uu * 2 + cc) * 128
            if half is None:
                return buf.at[pl.ds(pl.multiple_of(start, 128), 128), :]
            return buf.at[pl.ds(pl.multiple_of(start + half * 64, 64), 64), :]

        def mark(xx, uu, cc, half=None):
            return sem_w.at[bank * 32 + (xx * 4 + uu * 2 + cc) * 2 + (half or 0)]

        def send(who, key, to, half=None):
            post(lambda: (block(*key, half), block(*key, half), mark(*key, half)), to, who)

        def wait(key, half=None):
            arrived(block(*key, half), mark(*key, half))

        def own():
            @pl.when(source)
            def _():
                buf[pl.ds(pl.multiple_of(row * 128, 128), 128), :] = serve[...]

            @pl.when(jnp.logical_not(source))
            def _():
                post(lambda: (serve, block(x, u, c), sem_own.at[bank]), to_core, "receiver")

        def start():
            @pl.when(source)
            def _():
                arrived(block(x, u, 1 - c), sem_own.at[bank])
                for cc, order in ((0, (to_xp, to_xn, to_ya, to_yb)), (1, (to_ya, to_yb, to_xp, to_xn))):
                    for to in order:
                        send("source", (x, u, cc), to)

        def early():
            @pl.when(source)
            def _():
                me = "source"
                wait((xn, u, 0))
                send(me, (xn, u, 0), to_xp, 0)
                send(me, (xn, u, 0), to_ya)
                send(me, (xn, u, 0), to_yb)
                wait((xp, u, 0))
                send(me, (xp, u, 0), to_xn, 1)
                send(me, (xp, u, 0), to_ya)
                send(me, (xp, u, 0), to_yb)
                wait((x, v, 1))
                send(me, (x, v, 1), to_yb, 1)
                send(me, (x, v, 1), to_xp)
                send(me, (x, v, 1), to_xn)
                wait((xn, u, 1))
                send(me, (xn, u, 1), to_xp, 0)
                wait((xp, u, 1))
                send(me, (xp, u, 1), to_xn, 1)
                wait((xo, u, 0), 0)
                wait((xo, u, 0), 1)
                send(me, (xo, u, 0), to_ya)
                send(me, (xo, u, 0), to_yb)

            @pl.when(jnp.logical_not(source))
            def _():
                me = "receiver"
                wait((x, v, 1))
                send(me, (x, v, 1), to_ya, 0)
                send(me, (x, v, 1), to_xp)
                send(me, (x, v, 1), to_xn)
                wait((x, v, 0))
                wait((xn, v, 0))
                send(me, (xn, v, 0), to_ya)
                wait((xp, v, 0))
                send(me, (xp, v, 0), to_ya)
                wait((x, u, 1), 0)
                wait((x, u, 1), 1)
                send(me, (x, u, 1), to_xp)
                send(me, (x, u, 1), to_xn)
                wait((xn, v, 1))
                send(me, (xn, v, 1), to_xp, 0)
                wait((xp, v, 1))
                send(me, (xp, v, 1), to_xn, 1)

        def late(i):
            @pl.when(source)
            def _():
                me = "source"
                wait((xs[i], v, 0))
                if i in (0, 3):
                    send(me, (xs[i], v, 0), to_yb)
                if i == 1:
                    wait((xn, v, 1))
                    send(me, (xn, v, 1), to_xp, 0)
                if i == 2:
                    wait((xp, v, 1))
                    send(me, (xp, v, 1), to_xn, 1)
                if i == 3:
                    for uu in (u, v):
                        wait((xo, uu, 1), 0)
                        wait((xo, uu, 1), 1)

            @pl.when(jnp.logical_not(source))
            def _():
                me = "receiver"
                if i == 1:
                    wait((xn, u, 1))
                    send(me, (xn, u, 1), to_xp, 0)
                if i == 2:
                    wait((xp, u, 1))
                    send(me, (xp, u, 1), to_xn, 1)
                wait((xs[i], u, 0))
                if i == 3:
                    wait((xo, v, 0))
                    for uu in (v, u):
                        wait((xo, uu, 1), 0)
                        wait((xo, uu, 1), 1)

        return own, start, early, late

    own_q, start_q, early_q, late_q = weights(gq, srvq, 0)
    own_o, start_o, early_o, late_o = weights(go, srvo, 1)
    own_f, start_f, early_f, late_f = weights(gf, srvf, 2)

    exchanged(srvq, 0)
    own_q()

    @pl.when(jnp.logical_not(source))
    def _():
        arrived(xg.at[:, lanes(mine)], sem_swap.at[0])

    start_q()
    gather_start(xg, 0, TOK, 0)
    exchanged(srvo, 1)
    own_o()
    exchanged(srvf, 2)
    own_f()
    oq[...] = srvq[...]
    oo[...] = srvo[...]
    of[...] = srvf[...]
    early_q()
    gather_near(xg, 0, TOK, 0)
    gather_far(xg, 0, TOK, 0)
    start_o()
    gather_core(xg, 0, TOK, 0)

    def scales(buf, first):
        @pl.loop(0, S // 128)
        def _(i):
            rows = pl.ds(pl.multiple_of(first + i * 128, 128), 128)
            tokens = buf[rows, :].astype(F32)
            total = jnp.sum(tokens * tokens, axis=1, keepdims=True)
            scl[rows, :] = jnp.broadcast_to(lax.rsqrt(total * (1.0 / D) + EPS), (128, 128))

    scales(xg, 0)
    scales(xg, S)

    for i, xx in enumerate((x, xn, xp, xo)):
        late_q(i)
        feats = pl.ds(pl.multiple_of(xx * 512, 512), 512)

        @pl.loop(0, WIDE // 256)
        def _(n):
            wide = pl.ds(pl.multiple_of(n * 256, 256), 256)
            for m in range(REQS):
                rows = pl.ds(m * S, S)
                term = jnp.dot(xg[rows, feats], gq[feats, wide], preferred_element_type=F32)
                if i == 0:
                    acc[rows, wide] = term
                else:
                    acc[rows, wide] += term

    def retention(r):
        first = r * S
        rows = pl.ds(first, S)
        scale = scl[rows, :]
        for ref, at, gain in ((qs, 0, 1.0), (ks, KEY, 1.0 / math.sqrt(KEY))):
            a = (acc[rows, at : at + 128] * scale).astype(BF).astype(F32)
            b = (acc[rows, at + 128 : at + 256] * scale).astype(BF).astype(F32)
            ref[:, 0:128] = ((a * cosr[...] - b * sinr[...]) * gain).astype(BF)
            ref[:, 128:256] = ((a * sinr[...] + b * cosr[...]) * gain).astype(BF)
        wide_scale = jnp.concatenate([scale] * 4, axis=1)
        value = (acc[rows, 512:1024] * wide_scale).astype(BF)
        for t in range(S // BLOCK):
            q = qs[t * BLOCK : (t + 1) * BLOCK, :]
            total = jnp.zeros((BLOCK, VAL), F32)
            denom = jnp.zeros((BLOCK, 1), F32)
            for s in range(t + 1):
                k = ks[s * BLOCK : (s + 1) * BLOCK, :]
                score = lax.dot_general(q, k, NT, preferred_element_type=F32)
                score = score * (near[...] if s == t else far[...])
                denom += jnp.sum(score, axis=1, keepdims=True)
                total += jnp.dot(
                    score.astype(BF),
                    value[s * BLOCK : (s + 1) * BLOCK, :],
                    preferred_element_type=F32,
                )
            kept = total / jnp.maximum(jnp.abs(denom), 1.0)
            centred = kept - jnp.mean(kept, axis=1, keepdims=True)
            spread = jnp.mean(centred * centred, axis=1, keepdims=True)
            block = pl.ds(first + t * BLOCK, BLOCK)
            gate = (acc[block, 1024:1536] * wide_scale[t * BLOCK : (t + 1) * BLOCK, :]).astype(BF)
            mixed[block, :] = (
                jax.nn.silu(gate.astype(F32)) * (centred * lax.rsqrt(spread + EPS))
            ).astype(BF)

    def terms(left, weight, at, r, bank):
        rows = pl.ds(r * S, S)
        base = count[0]
        count[0] += 4
        copies = []

        def term(slot):
            feats = pl.ds(pl.multiple_of(slot * FEAT, FEAT), FEAT)
            part[r, slot] = lax.dot_general(
                left[rows, :], weight[feats, at : at + 512], NT, preferred_element_type=F32
            ).astype(BF)

        def to_other(j):
            zz = lax.rem(zo + j, 4)
            slot = (1 - c) * 4 + zz
            return pltpu.make_async_remote_copy(
                src_ref=part.at[r, slot],
                dst_ref=pairs.at[bank, r, zz],
                send_sem=send_sem.at[base + j],
                recv_sem=sem_core.at[bank * 8 + r * 4 + zz],
                device_id=to_core,
                device_id_type=MESH,
            )

        @pl.loop(0, 4)
        def _(j):
            term((1 - c) * 4 + lax.rem(zo + j, 4))
            to_other(j).start()

        @pl.loop(0, 4)
        def _(j):
            term(c * 4 + lax.rem(zo + j, 4))

        def sent():
            @pl.loop(0, 4)
            def _(j):
                to_other(j).wait_send()

        return sent

    HALF = S // 2
    TOP, BOT = pl.ds(0, HALF), pl.ds(HALF, HALF)

    def pair(r, bank, zz):
        arrived(pairs.at[bank, r, zz], sem_core.at[bank * 8 + r * 4 + zz])
        slot = c * 4 + zz
        return slot

    def both(r, bank, zz, rows):
        return part[r, c * 4 + zz, rows, :].astype(F32) + pairs[bank, r, zz, rows, :].astype(F32)

    def reduce_start(r, bank):
        base = (bank * 2 + r) * 4
        rel = (bank * 2 + r) * 2
        slot = pair(r, bank, zo)
        part[r, slot] = both(r, bank, zo, pl.ds(0, S)).astype(BF)
        post(lambda slot=slot: (part.at[r, slot, TOP, :], relay.at[bank, r, 0], sem_rel.at[rel]), to_zp)
        post(lambda slot=slot: (part.at[r, slot, BOT, :], relay.at[bank, r, 1], sem_rel.at[rel + 1]), to_zn)
        slot = pair(r, bank, zp)
        part[r, slot, BOT, :] = both(r, bank, zp, BOT).astype(BF)
        post(lambda slot=slot: (part.at[r, slot, BOT, :], final.at[bank, r, 0, BOT, :], sem_fin.at[base + 1]), to_zp)
        slot = pair(r, bank, zn)
        part[r, slot, TOP, :] = both(r, bank, zn, TOP).astype(BF)
        post(lambda slot=slot: (part.at[r, slot, TOP, :], final.at[bank, r, 1, TOP, :], sem_fin.at[base + 2]), to_zn)

    def reduce_relay(r, bank):
        base = (bank * 2 + r) * 4
        rel = (bank * 2 + r) * 2
        arrived(relay.at[bank, r, 0], sem_rel.at[rel])
        slot = c * 4 + zp
        part[r, slot, TOP, :] = (both(r, bank, zp, TOP) + relay[bank, r, 0].astype(F32)).astype(BF)
        post(lambda slot=slot: (part.at[r, slot, TOP, :], final.at[bank, r, 0, TOP, :], sem_fin.at[base]), to_zp)
        arrived(relay.at[bank, r, 1], sem_rel.at[rel + 1])
        slot = c * 4 + zn
        part[r, slot, BOT, :] = (both(r, bank, zn, BOT) + relay[bank, r, 1].astype(F32)).astype(BF)
        post(lambda slot=slot: (part.at[r, slot, BOT, :], final.at[bank, r, 1, BOT, :], sem_fin.at[base + 3]), to_zn)
        pair(r, bank, z)

    def reduce_end(r, bank):
        base = (bank * 2 + r) * 4
        arrived(final.at[bank, r, 0, BOT, :], sem_fin.at[base + 1])
        arrived(final.at[bank, r, 1, TOP, :], sem_fin.at[base + 2])
        arrived(final.at[bank, r, 0, TOP, :], sem_fin.at[base])
        arrived(final.at[bank, r, 1, BOT, :], sem_fin.at[base + 3])
        return (
            both(r, bank, z, pl.ds(0, S))
            + final[bank, r, 0].astype(F32)
            + final[bank, r, 1].astype(F32)
        )

    def add_residual(r):
        rows = pl.ds(r * S, S)
        total = xg[rows, lanes(mine)].astype(F32) + reduce_end(r, 0)
        resid[rows, :] = total
        xm[rows, lanes(mine)] = total.astype(BF)

    def feed(r):
        rows = pl.ds(r * S, S)
        scales(xm, r * S)
        scale = jnp.concatenate([scl[rows, :]] * 2, axis=1)

        @pl.loop(0, 2)
        def _(n):
            at = pl.ds(pl.multiple_of(n * 256, 256), 256)
            up_at = pl.ds(pl.multiple_of(512 + n * 256, 256), 256)
            gate = jnp.dot(xm[rows, :], gf[:, at], preferred_element_type=F32) * scale
            up = jnp.dot(xm[rows, :], gf[:, up_at], preferred_element_type=F32) * scale
            hidden[rows, at] = (jax.nn.silu(gate) * up).astype(BF)

    def finish(r):
        rows = pl.ds(r * S, S)
        outb[rows, :] = (resid[rows, :] + reduce_end(r, 1)).astype(BF)

        @pl.when(jnp.logical_not(source))
        def _():
            post(
                lambda: (outb.at[rows, :], swapb.at[rows, :], sem_swap.at[1 + r]),
                to_swap,
                "receiver",
            )

    retention(0)
    early_o()
    start_f()
    retention(1)
    for i in range(4):
        late_o(i)
    sent = []
    sent.append(terms(mixed, go, 0, 0, 0))
    early_f()
    sent.append(terms(mixed, go, 0, 1, 0))
    reduce_start(0, 0)
    late_f(0)
    reduce_relay(0, 0)
    reduce_start(1, 0)
    late_f(1)
    reduce_relay(1, 0)
    add_residual(0)
    gather_start(xm, 0, S, 1)
    late_f(2)
    add_residual(1)
    gather_start(xm, S, S, 2)
    late_f(3)
    gather_near(xm, 0, S, 1)
    gather_far(xm, 0, S, 1)
    gather_near(xm, S, S, 2)
    gather_core(xm, 0, S, 1)
    feed(0)
    gather_far(xm, S, S, 2)

    for one in sent:
        one()
    for when, copy in pending:
        assert when in (None, "source", "receiver")
    plain = [copy for when, copy in pending if when is None]
    for copy in plain:
        copy().wait_send()
    pending[:] = [(when, copy) for when, copy in pending if when is not None]

    last = [terms(hidden, gf, 1024, 0, 1)]
    gather_core(xm, S, S, 2)
    reduce_start(0, 1)
    feed(1)
    reduce_relay(0, 1)
    last.append(terms(hidden, gf, 1024, 1, 1))
    reduce_start(1, 1)
    finish(0)
    reduce_relay(1, 1)
    finish(1)

    @pl.when(source)
    def _():
        y[...] = outb[...]

    @pl.when(jnp.logical_not(source))
    def _():
        for r in range(REQS):
            rows = pl.ds(r * S, S)
            arrived(swapb.at[rows, :], sem_swap.at[1 + r])
        y[...] = swapb[...]

    for one in last:
        one()
    for when, copy in pending:
        if when is None:
            copy().wait_send()

    @pl.when(source)
    def _():
        for when, copy in pending:
            if when == "source":
                copy().wait_send()

    @pl.when(jnp.logical_not(source))
    def _():
        for when, copy in pending:
            if when == "receiver":
                copy().wait_send()


def layer(hidden, qkvg, gateup, out_t, down_t):
    cosine, sine = tables()
    vmem = pl.BlockSpec(memory_space=pltpu.VMEM)
    dma = pltpu.SemaphoreType.DMA
    scratch = [
        pltpu.VMEM((8, 16, WIDE), BF),
        pltpu.VMEM((8, 16, 512), BF),
        pltpu.VMEM((8, 16, 1536), BF),
        pltpu.VMEM((128, WIDE), BF),
        pltpu.VMEM((128, 512), BF),
        pltpu.VMEM((128, 1536), BF),
        pltpu.VMEM((TOK, D), BF),
        pltpu.VMEM((TOK, D), BF),
        pltpu.VMEM((D, WIDE), BF),
        pltpu.VMEM((D, 512), BF),
        pltpu.VMEM((D, 1536), BF),
        pltpu.VMEM((TOK, WIDE), F32),
        pltpu.VMEM((TOK, 128), F32),
        pltpu.VMEM((BLOCK, BLOCK), F32),
        pltpu.VMEM((BLOCK, BLOCK), F32),
        pltpu.VMEM((S, KEY), BF),
        pltpu.VMEM((S, KEY), BF),
        pltpu.VMEM((TOK, VAL), BF),
        pltpu.VMEM((TOK, 512), BF),
        pltpu.VMEM((REQS, 8, S, FEAT), BF),
        pltpu.VMEM((2, REQS, 4, S, FEAT), BF),
        pltpu.VMEM((2, REQS, 2, S // 2, FEAT), BF),
        pltpu.VMEM((2, REQS, 2, S, FEAT), BF),
        pltpu.VMEM((TOK, FEAT), F32),
        pltpu.VMEM((TOK, FEAT), BF),
        pltpu.VMEM((TOK, FEAT), BF),
        dma((256,)),
        dma((24,)),
        dma((3,)),
        dma((96,)),
        dma((48,)),
        dma((16,)),
        dma((8,)),
        dma((16,)),
        dma((3,)),
        dma((1,)),
    ]
    return pl.pallas_call(
        kernel,
        out_shape=(
            jax.ShapeDtypeStruct((TOK, FEAT), BF),
            jax.ShapeDtypeStruct((128, WIDE), BF),
            jax.ShapeDtypeStruct((128, 1536), BF),
            jax.ShapeDtypeStruct((128, 512), BF),
        ),
        in_specs=[vmem] * 7,
        out_specs=(vmem,) * 4,
        scratch_shapes=scratch,
        compiler_params=pltpu.CompilerParams(
            collective_id=0, has_side_effects=True, vmem_limit_bytes=62 * 1024 * 1024
        ),
    )(hidden, qkvg, gateup, out_t, down_t, jnp.asarray(cosine), jnp.asarray(sine))


def shards(hidden_states, lengths, qkvg_master, gateup_master, out_master, down_master):
    y, wq, wf, wo = layer(
        hidden_states, qkvg_master, gateup_master, out_master.T, down_master.T
    )
    live = jnp.arange(S)[None, :] < lengths[:, None]
    output = jnp.where(live.reshape(TOK, 1), y, jnp.zeros_like(y))
    gateup = jnp.stack([wf[:, 0:512], wf[:, 512:1024]])
    return (output, wq, gateup, wo.T, wf[:, 1024:1536].T)


def solution(mesh):
    return jax.shard_map(
        shards,
        mesh=mesh,
        in_specs=(
            P("row", "col"),
            P("row"),
            P(("row", "col"), None),
            P(None, ("row", "col"), None),
            P(None, ("row", "col")),
            P(None, ("row", "col")),
        ),
        out_specs=(
            P("row", "col"),
            P("row", "col"),
            P(None, "row", "col"),
            P("col", "row"),
            P("col", "row"),
        ),
        check_vma=False,
    )
```

time: 547 us -> 184 us (0.34)
  waiting for transfers between devices: 282 us -> 0 us
  Pallas kernels: 0 us -> 177 us
  other arithmetic: 84 us -> 2.9 us
  blocking collectives: 61.6 us -> 0 us
  local copies, waits for them, and re-layouts: 53.3 us -> 2.97 us
  matrix products: 46 us -> 0 us
  between operations: 14.5 us -> 0.68 us
    pallas_call x0 -> x1, Pallas kernels: none -> 177 us  [layer(): pl.pallas_call(kernel, out_shape=(jax.ShapeDtypeStruct((TOK, FEAT), BF),...]
    reduce_scatter x2 -> x0, waiting for transfers between devices: 140 us -> none  [the longest x1 81.1 us: shards(): lax.psum_scatter(partial_feed.astype(jnp.bfloat16), 'col', scatter_dimens...]
    all_gather x6 -> x0, waiting for transfers between devices: 136 us -> none  [the longest x1 75.5 us: shards(): normed_mid = lax.all_gather(normed_share, 'col', axis=1, tiled=True)]
    unnamed x5 -> x0, other arithmetic: 67 us -> none
    dot_general x14 -> x0, matrix products: 46 us -> none  [the longest x1 10.5 us: shards(): jnp.dot(columns, lax.all_gather(qkvg_blocks, 'row', axis=0, tiled=True),...]
    all_to_all x3 -> x0, blocking collectives: 44.6 us -> none  [the longest x1 16.9 us: shards(): lax.all_to_all(qkvg_master.astype(jnp.bfloat16)[None], 'col', split_axis=...]
    psum x1 -> x0, blocking collectives: 17 us -> none  [shards(): squares = lax.psum(jnp.sum(residual * residual, axis=1), 'col')]
    all_to_all x6 -> x0, local copies, waits for them, and re-layouts: 16.2 us -> none  [the longest x3 12.3 us: shards(): lax.all_to_all(qkvg_master.astype(jnp.bfloat16)[None], 'col', split_axis=...]
  transfers between devices with their start and end apart: 9 -> 0, of which waited for: 8 -> 0; matrix products, arithmetic and copies ran while one was open for 30% -> 0% of each run, Pallas kernels for 0% -> 0%
where the time goes in v1:
time: 184 us
  Pallas kernels  177 us (96%)
  local copies, waits for them, and re-layouts  2.97 us (2%)
  other arithmetic  2.9 us (2%)
    pallas_call x1, Pallas kernels, layer(): pl.pallas_call(kernel, out_shape=(jax.ShapeDtypeStruct((TOK, FEAT), BF),...  177 us

profile of v1, /device:TPU:1, one launch (start us, length us, event | category | flops | bytes accessed | tf_op | source)
XLA Modules:
  0.0 183.7 jit_solution(1519492731254032112)
XLA Ops:
  0.6 0.0 copy-start.3
  0.6 0.6 copy-done.3
  1.3 0.1 iota_compare_fusion
  1.4 177.2 %shard_map.119 = (bf16[1024,256]{1,0:T(8,128)(2,1)}, bf16[128,1536]{1,0:T(8,128)(2,1)}, bf16[128,1536]{1,0:T(8,128)(2,1)}, bf16[128,512]{1,0:T(8,128)(2,1)}) custom-call(bf16[1024,256]{1,0:T(8,128)(2,1)} %hid.1, f32[16,12288]{1,0:T(8,128)} %qm.1, f32[2,16,4096]{2,1,0:T(8,128)} %gm.1, f32[16,4096]{1,0:T(8,128)} %bitcast.9, f32[16,4096]{1,0:T(8,128)} %bitcast.10, ...), custom_call_target="tpu_custom_call" | custom-call | tf_op jit(solution)/shard_map/pallas_call | solution.py:643
  178.5 0.0 copy-start.2
  178.6 0.0 copy-start.1
  178.6 2.1 %broadcast_select_fusion = bf16[1024,256]{1,0:T(8,128)(2,1)} fusion(bf16[1024,256]{1,0:T(8,128)(2,1)} %get-tuple-element.9, pred[1024]{0:T(1024)(128)(4,1)S(1)} %lt.23), kind=kLoop, calls=%fused_computation | loop fusion | flops 262144 | bytes 1049600 | tf_op jit(solution)/shard_map/jit(_where)/select_n | solution.py:665
  180.7 0.0 copy-done.2
  180.7 0.8 copy.13
  181.4 0.0 copy-done.1
  181.5 0.0 copy-start
  181.5 0.8 copy.14
  182.2 0.7 pad_maximum_fusion
  183.0 0.0 copy-done
  183.0 0.7 copy.16
  (2 shorter events, 0.0 us)
Async XLA Ops:
  0.6 0.7 copy-start.3
  178.5 2.1 %copy-start.2 = (bf16[128,512]{1,0:T(8,128)(2,1)S(1)}, bf16[128,512]{1,0:T(8,128)(2,1)}, u32[]{:S(2)}) copy-start(bf16[128,512]{1,0:T(8,128)(2,1)} %get-tuple-element.12) | copy-start | bytes 393220
  178.6 2.9 %copy-start.1 = (bf16[128,1536]{1,0:T(8,128)(2,1)S(1)}, bf16[128,1536]{1,0:T(8,128)(2,1)}, u32[]{:S(2)}) copy-start(bf16[128,1536]{1,0:T(8,128)(2,1)} %get-tuple-element.11) | copy-start | bytes 1179652
  181.5 1.5 copy-start

commit v2 on v1

v2 whole, which is shorter than its diff:
```python
import math

import jax
import jax.numpy as jnp
import numpy as np
from jax import lax
from jax.experimental import pallas as pl
from jax.experimental.pallas import tpu as pltpu
from jax.sharding import PartitionSpec as P

D = 2048
HEADS = 8
KEY = 256
VAL = 512
S = 512
BLOCK = 256
FF = 4096
WIDE = 2 * KEY + 2 * VAL
TOK = 1024
FEAT = 256
REQS = 2
EPS = 1e-05
MESH = pl.DeviceIdType.MESH
BF = jnp.bfloat16
F32 = jnp.float32
NT = (((1,), (1,)), ((), ()))


def tables():
    half = KEY // 2
    freq = np.power(np.float32(10000.0), (-2.0 * np.arange(half) / KEY).astype(np.float32))
    angle = np.arange(S, dtype=np.float32)[:, None] * freq.astype(np.float32)[None, :]
    return np.cos(angle).astype(np.float32), np.sin(angle).astype(np.float32)


def kernel(
    lens, hid, qm_hbm, gm_hbm, om_hbm, dm_hbm, cos_hbm, sin_hbm,
    y, oq, of, om_out, od_out,
    qm, gm, om, dm, cosr, sinr, turned,
    sbq, sbo, sbf, srvq, srvo, srvf,
    xg, xm, gq, go, gf, acc, scl, near, far, qs, ks, mixed, hidden,
    part, pairs, relay, final, resid, outb, swapb,
    send_sem, sem_a2a, sem_own, sem_w, sem_x, sem_core, sem_rel, sem_fin, sem_swap, loc_sem,
):
    row = lax.axis_index("row")
    col = lax.axis_index("col")
    x = lax.div(row, 4)
    u = lax.rem(lax.div(row, 2), 2)
    c = lax.rem(row, 2)
    h = lax.div(col, 4)
    z = lax.rem(col, 4)
    xp, xn, xo = lax.rem(x + 1, 4), lax.rem(x + 3, 4), lax.rem(x + 2, 4)
    zp, zn, zo = lax.rem(z + 1, 4), lax.rem(z + 3, 4), lax.rem(z + 2, 4)
    source = c == h
    mine = c * 4 + z
    yy = h * 2 + u
    yp, yn, yo = lax.rem(yy + 1, 4), lax.rem(yy + 3, 4), lax.rem(yy + 2, 4)

    def device(xx, uu, cc, hh, zz):
        return (xx * 4 + uu * 2 + cc, hh * 4 + zz)

    to_core = device(x, u, 1 - c, h, z)
    to_swap = device(x, u, h, c, z)
    to_xp, to_xn = device(xp, u, c, h, z), device(xn, u, c, h, z)
    to_zp, to_zn = device(x, u, c, h, zp), device(x, u, c, h, zn)
    to_yp = device(x, lax.rem(yp, 2), c, lax.div(yp, 2), z)
    to_yn = device(x, lax.rem(yn, 2), c, lax.div(yn, 2), z)

    def post(src, dst, sent, recv, target):
        pltpu.make_async_remote_copy(
            src_ref=src,
            dst_ref=dst,
            send_sem=send_sem.at[sent],
            recv_sem=recv,
            device_id=target,
            device_id_type=MESH,
        ).start()

    def arrived(ref, recv):
        pltpu.make_async_remote_copy(
            src_ref=ref,
            dst_ref=ref,
            send_sem=send_sem.at[0],
            recv_sem=recv,
            device_id=to_core,
            device_id_type=MESH,
        ).wait_recv()

    def gone(ref, sent):
        pltpu.make_async_remote_copy(
            src_ref=ref,
            dst_ref=ref,
            send_sem=send_sem.at[sent],
            recv_sem=sem_swap.at[0],
            device_id=to_core,
            device_id_type=MESH,
        ).wait_send()

    loads = [
        pltpu.make_async_copy(src, dst, loc_sem.at[i])
        for i, (src, dst) in enumerate(
            ((qm_hbm, qm), (om_hbm, om), (gm_hbm, gm), (dm_hbm, dm), (cos_hbm, cosr), (sin_hbm, sinr))
        )
    ]
    for one in loads:
        one.start()

    barrier = pltpu.get_barrier_semaphore()
    others = [lax.rem(mine + i, 8) for i in range(1, 8)]
    peers = [device(x, u, lax.div(other, 4), h, lax.rem(other, 4)) for other in others]
    swap_peer = device(x, u, 1 - c, 1 - h, z)
    greet = peers + [swap_peer, to_xp, to_xn, to_yp, to_yn]
    for peer in greet:
        pl.semaphore_signal(barrier, inc=1, device_id=peer, device_id_type=MESH)
    loads[0].wait()
    for i in range(8):
        sbq[i] = qm[:, i * WIDE : (i + 1) * WIDE].astype(BF)
    pl.semaphore_wait(barrier, len(greet))

    def dealt(buf, cc, zz, lo, width):
        start = (x * 4 + u * 2 + cc) * 128 + h * 64 + zz * 16
        return buf.at[pl.ds(pl.multiple_of(start, 16), 16), pl.ds(lo, width)]

    def exchange(send, buf, group, lo, width):
        for i in range(1, 8):
            other = lax.rem(mine + i, 8)
            post(
                send.at[other],
                dealt(buf, c, z, lo, width),
                group,
                sem_a2a.at[group],
                device(x, u, lax.div(other, 4), h, lax.rem(other, 4)),
            )
        start = (x * 4 + u * 2 + c) * 128 + h * 64 + z * 16
        buf[pl.ds(pl.multiple_of(start, 16), 16), lo : lo + width] = send[mine]

    def exchanged(buf, group, lo, width):
        arrived(buf.at[0:112, lo : lo + width], sem_a2a.at[group])

    exchange(sbq, gq, 0, 0, WIDE)

    def lanes(slot):
        return pl.ds(pl.multiple_of(slot * FEAT, FEAT), FEAT)

    def start_swap():
        @pl.when(jnp.logical_not(source))
        def _():
            post(hid, xg.at[:, lanes(col)], 3, sem_swap.at[0], to_swap)

        @pl.when(source)
        def _():
            pltpu.make_async_copy(hid, xg.at[:, lanes(col)], loc_sem.at[6]).start()

    def end_swap():
        @pl.when(jnp.logical_not(source))
        def _():
            arrived(xg.at[:, lanes(mine)], sem_swap.at[0])

        @pl.when(source)
        def _():
            pltpu.make_async_copy(hid, xg.at[:, lanes(col)], loc_sem.at[6]).wait()

    start_swap()

    for one in loads[1:]:
        one.wait()
    for i in range(8):
        sbo[i] = om[:, i * VAL : (i + 1) * VAL].astype(BF)
        sbf[i, :, 0:512] = gm[0, :, i * 512 : (i + 1) * 512].astype(BF)
        sbf[i, :, 512:1024] = gm[1, :, i * 512 : (i + 1) * 512].astype(BF)
        sbf[i, :, 1024:1536] = dm[:, i * 512 : (i + 1) * 512].astype(BF)
    exchange(sbo, go, 1, 0, 512)
    exchange(sbf, gf, 2, 0, 1536)

    head = c * 4 + z
    rate = jnp.float32(0.0)
    for i in range(HEADS):
        rate = jnp.where(head == i, jnp.float32(math.log1p(-(2.0 ** (-5 - i)))), rate)
    lag = lax.broadcasted_iota(jnp.int32, (BLOCK, BLOCK), 0) - lax.broadcasted_iota(
        jnp.int32, (BLOCK, BLOCK), 1
    )
    near[...] = jnp.where(lag >= 0, jnp.exp(jnp.maximum(lag, 0).astype(F32) * rate), 0.0)
    far[...] = jnp.exp((lag + BLOCK).astype(F32) * rate)

    def act_ref(buf, rows, slot):
        return buf.at[rows, lanes(slot)]

    def gather_post(buf, rows, slot, bank, kind, to):
        ref = act_ref(buf, rows, slot)
        post(ref, ref, 4 + bank, sem_x.at[bank * 4 + kind], to)

    def gather_start(buf, first, size, bank):
        rows = pl.ds(first, size)
        gather_post(buf, rows, mine, bank, 0, to_zp)
        gather_post(buf, rows, mine, bank, 1, to_zn)
        gather_post(buf, rows, mine, bank, 3, to_core)

    def gather_near(buf, first, size, bank):
        rows = pl.ds(first, size)
        half = size // 2
        for kind, zz, start, to in ((0, zn, first, to_zp), (1, zp, first + half, to_zn)):
            slot = c * 4 + zz
            arrived(act_ref(buf, rows, slot), sem_x.at[bank * 4 + kind])
            gather_post(buf, pl.ds(start, half), slot, bank, 2, to)
            gather_post(buf, rows, slot, bank, 3, to_core)

    def gather_far(buf, first, size, bank):
        rows = pl.ds(first, size)
        slot = c * 4 + zo
        arrived(act_ref(buf, rows, slot), sem_x.at[bank * 4 + 2])
        gather_post(buf, rows, slot, bank, 3, to_core)

    def gather_core(buf, first, size, bank):
        theirs = pl.ds(pl.multiple_of((1 - c) * 1024, 1024), 1024)
        arrived(buf.at[pl.ds(first, size), theirs], sem_x.at[bank * 4 + 3])

    def gather_gone(buf, first, size, bank):
        gone(buf.at[pl.ds(first, size), 0 : 7 * FEAT], 4 + bank)

    def weights(buf, bank, lo, width):
        xs, ys = (x, xn, xp, xo), (yy, yn, yp, yo)
        cut = pl.ds(lo, width)

        def block(key, half=None):
            xx, where, cc = key
            start = (xx * 4 + lax.rem(where, 2) * 2 + cc) * 128 + lax.div(where, 2) * 64
            if half is None:
                return buf.at[pl.ds(pl.multiple_of(start, 64), 64), cut]
            return buf.at[pl.ds(pl.multiple_of(start + half * 32, 32), 32), cut]

        def send(key, to, kind, half=None):
            ref = block(key, half)
            post(ref, ref, 7 + bank, sem_w.at[bank * 19 + kind], to)

        def wait(key, kind):
            arrived(block(key), sem_w.at[bank * 19 + kind])

        def start():
            for to, kind in ((to_xp, 0), (to_xn, 2), (to_yp, 6), (to_yn, 6)):
                send((x, yy, 0), to, kind)
            for to, kind in ((to_yp, 1), (to_yn, 3), (to_xp, 10), (to_xn, 10)):
                send((x, yy, 1), to, kind)

        def early(i):
            key = (
                (xn, yy, 0), (x, yn, 1), (xp, yy, 0), (x, yp, 1), (xo, yy, 0), (x, yo, 1)
            )[i]
            wait(key, i)
            if i < 4:
                send(key, (to_xp, to_yp, to_xn, to_yn)[i], 4 + i % 2, i // 2)
            place = i // 2 + 1
            if i % 2 == 0:
                send(key, to_yp, 6 + place)
                send(key, to_yn, 6 + place)
            else:
                send(key, to_xp, 10 + place)
                send(key, to_xn, 10 + place)

        def late(i):
            arrived(buf.at[0:128, cut], sem_w.at[bank * 19 + 6 + i])
            if i in (0, 3):
                send((xs[i], yn, 0), to_yp, 14 + i)
            else:
                send((xs[i], yp, 0), to_yn, 14 + i)
            arrived(buf.at[0:128, cut], sem_w.at[bank * 19 + 10 + i])
            if i in (0, 3):
                send((xn, ys[i], 1), to_xp, 18)
            else:
                send((xp, ys[i], 1), to_xn, 18)

        def last(i):
            wait((xs[i], yo, 0), 14 + i)
            if i == 3:
                arrived(buf.at[0:256, cut], sem_w.at[bank * 19 + 18])

        def left():
            gone(buf.at[0:1920, cut], 7 + bank)

        return start, early, late, last, left

    start_q, early_q, late_q, last_q, left_q = weights(gq, 0, 0, WIDE)
    start_o, early_o, late_o, last_o, left_o = weights(go, 1, 0, 512)
    start_g, early_g, late_g, last_g, left_g = weights(gf, 2, 0, 1024)
    start_d, early_d, late_d, last_d, left_d = weights(gf, 3, 1024, 512)

    def serve_start():
        theirs = pl.ds(pl.multiple_of((x * 4 + u * 2 + 1 - c) * 128, 128), 128)
        ours = pl.ds(pl.multiple_of(row * 128, 128), 128)

        @pl.when(source)
        def _():
            for i, (buf, srv) in enumerate(((gq, srvq), (go, srvo), (gf, srvf))):
                post(buf.at[theirs, :], srv, 11 + i, sem_own.at[i], to_core)
                srv[...] = buf[ours, :]

    def serve_end():
        @pl.when(jnp.logical_not(source))
        def _():
            for i, srv in enumerate((srvq, srvo, srvf)):
                arrived(srv, sem_own.at[i])

        store_weights()

    def stores():
        return [
            pltpu.make_async_copy(srvq, oq, loc_sem.at[7]),
            pltpu.make_async_copy(srvf.at[:, 0:512], of.at[0], loc_sem.at[8]),
            pltpu.make_async_copy(srvf.at[:, 512:1024], of.at[1], loc_sem.at[9]),
            pltpu.make_async_copy(turned.at[0], om_out, loc_sem.at[10]),
            pltpu.make_async_copy(turned.at[1], od_out, loc_sem.at[11]),
        ]

    def store_weights():
        turned[0] = jnp.transpose(srvo[...])
        turned[1] = jnp.transpose(srvf[:, 1024:1536])
        for one in stores():
            one.start()

    def scales(buf, first):
        @pl.loop(0, S // 128)
        def _(i):
            rows = pl.ds(pl.multiple_of(first + i * 128, 128), 128)
            tokens = buf[rows, :].astype(F32)
            total = jnp.sum(tokens * tokens, axis=1, keepdims=True)
            scl[rows, :] = jnp.broadcast_to(lax.rsqrt(total * (1.0 / D) + EPS), (128, 128))

    def project(i):
        feats = pl.ds(pl.multiple_of((x, xn, xp, xo)[i] * 512, 512), 512)

        @pl.loop(0, WIDE // 256)
        def _(n):
            wide = pl.ds(pl.multiple_of(n * 256, 256), 256)
            for m in range(REQS):
                rows = pl.ds(m * S, S)
                term = jnp.dot(xg[rows, feats], gq[feats, wide], preferred_element_type=F32)
                if i == 0:
                    acc[rows, wide] = term
                else:
                    acc[rows, wide] += term

    def retention(r):
        first = r * S
        rows = pl.ds(first, S)
        scale = scl[rows, :]
        for ref, at, gain in ((qs, 0, 1.0), (ks, KEY, 1.0 / math.sqrt(KEY))):
            a = (acc[rows, at : at + 128] * scale).astype(BF).astype(F32)
            b = (acc[rows, at + 128 : at + 256] * scale).astype(BF).astype(F32)
            ref[:, 0:128] = ((a * cosr[...] - b * sinr[...]) * gain).astype(BF)
            ref[:, 128:256] = ((a * sinr[...] + b * cosr[...]) * gain).astype(BF)
        wide_scale = jnp.concatenate([scale] * 4, axis=1)
        value = (acc[rows, 512:1024] * wide_scale).astype(BF)
        for t in range(S // BLOCK):
            q = qs[t * BLOCK : (t + 1) * BLOCK, :]
            total = jnp.zeros((BLOCK, VAL), F32)
            denom = jnp.zeros((BLOCK, 1), F32)
            for s in range(t + 1):
                k = ks[s * BLOCK : (s + 1) * BLOCK, :]
                score = lax.dot_general(q, k, NT, preferred_element_type=F32)
                score = score * (near[...] if s == t else far[...])
                denom += jnp.sum(score, axis=1, keepdims=True)
                total += jnp.dot(
                    score.astype(BF),
                    value[s * BLOCK : (s + 1) * BLOCK, :],
                    preferred_element_type=F32,
                )
            kept = total / jnp.maximum(jnp.abs(denom), 1.0)
            centred = kept - jnp.mean(kept, axis=1, keepdims=True)
            spread = jnp.mean(centred * centred, axis=1, keepdims=True)
            block = pl.ds(first + t * BLOCK, BLOCK)
            gate = (acc[block, 1024:1536] * wide_scale[t * BLOCK : (t + 1) * BLOCK, :]).astype(BF)
            mixed[block, :] = (
                jax.nn.silu(gate.astype(F32)) * (centred * lax.rsqrt(spread + EPS))
            ).astype(BF)

    def terms(left, weight, at, r, bank):
        rows = pl.ds(r * S, S)

        def term(slot):
            feats = pl.ds(pl.multiple_of(slot * FEAT, FEAT), FEAT)
            part[r, slot] = lax.dot_general(
                left[rows, :], weight[feats, at : at + 512], NT, preferred_element_type=F32
            ).astype(BF)

        @pl.loop(0, 4)
        def _(j):
            zz = lax.rem(zo + j, 4)
            slot = (1 - c) * 4 + zz
            term(slot)
            post(
                part.at[r, slot],
                pairs.at[bank, r, zz],
                14 + bank * 2 + r,
                sem_core.at[bank * 8 + r * 4 + zz],
                to_core,
            )

        @pl.loop(0, 4)
        def _(j):
            term(c * 4 + lax.rem(zo + j, 4))

    HALF = S // 2
    TOP, BOT = pl.ds(0, HALF), pl.ds(HALF, HALF)

    def pair(r, bank, zz):
        arrived(pairs.at[bank, r, zz], sem_core.at[bank * 8 + r * 4 + zz])
        slot = c * 4 + zz
        return slot

    def both(r, bank, zz, rows):
        return part[r, c * 4 + zz, rows, :].astype(F32) + pairs[bank, r, zz, rows, :].astype(F32)

    def reduce_start(r, bank):
        rel = (bank * 2 + r) * 2
        slot = pair(r, bank, zo)
        part[r, slot] = both(r, bank, zo, pl.ds(0, S)).astype(BF)
        post(part.at[r, slot, TOP, :], relay.at[bank, r, 0], 18 + bank * 2 + r, sem_rel.at[rel], to_zp)
        post(part.at[r, slot, BOT, :], relay.at[bank, r, 1], 18 + bank * 2 + r, sem_rel.at[rel + 1], to_zn)
        slot = pair(r, bank, zp)
        part[r, slot, BOT, :] = both(r, bank, zp, BOT).astype(BF)
        post(part.at[r, slot, BOT, :], final.at[bank, r, 0, BOT, :], 18 + bank * 2 + r, sem_fin.at[bank * 2 + r], to_zp)
        slot = pair(r, bank, zn)
        part[r, slot, TOP, :] = both(r, bank, zn, TOP).astype(BF)
        post(part.at[r, slot, TOP, :], final.at[bank, r, 1, TOP, :], 18 + bank * 2 + r, sem_fin.at[bank * 2 + r], to_zn)

    def reduce_relay(r, bank):
        rel = (bank * 2 + r) * 2
        arrived(relay.at[bank, r, 0], sem_rel.at[rel])
        slot = c * 4 + zp
        part[r, slot, TOP, :] = (both(r, bank, zp, TOP) + relay[bank, r, 0].astype(F32)).astype(BF)
        post(part.at[r, slot, TOP, :], final.at[bank, r, 0, TOP, :], 18 + bank * 2 + r, sem_fin.at[bank * 2 + r], to_zp)
        arrived(relay.at[bank, r, 1], sem_rel.at[rel + 1])
        slot = c * 4 + zn
        part[r, slot, BOT, :] = (both(r, bank, zn, BOT) + relay[bank, r, 1].astype(F32)).astype(BF)
        post(part.at[r, slot, BOT, :], final.at[bank, r, 1, BOT, :], 18 + bank * 2 + r, sem_fin.at[bank * 2 + r], to_zn)
        pair(r, bank, z)

    def reduce_end(r, bank):
        arrived(final.at[bank, r], sem_fin.at[bank * 2 + r])
        return (
            both(r, bank, z, pl.ds(0, S))
            + final[bank, r, 0].astype(F32)
            + final[bank, r, 1].astype(F32)
        )

    def reduce_gone(r, bank):
        gone(part.at[r, 0:4], 14 + bank * 2 + r)
        gone(part.at[r, 0:3], 18 + bank * 2 + r)

    def add_residual(r):
        rows = pl.ds(r * S, S)
        total = xg[rows, lanes(mine)].astype(F32) + reduce_end(r, 0)
        resid[rows, :] = total
        xm[rows, lanes(mine)] = total.astype(BF)

    def feed(r):
        rows = pl.ds(r * S, S)
        scales(xm, r * S)
        scale = jnp.concatenate([scl[rows, :]] * 2, axis=1)

        @pl.loop(0, 2)
        def _(n):
            at = pl.ds(pl.multiple_of(n * 256, 256), 256)
            up_at = pl.ds(pl.multiple_of(512 + n * 256, 256), 256)
            gate = jnp.dot(xm[rows, :], gf[:, at], preferred_element_type=F32) * scale
            up = jnp.dot(xm[rows, :], gf[:, up_at], preferred_element_type=F32) * scale
            hidden[rows, at] = (jax.nn.silu(gate) * up).astype(BF)

    def finish(r):
        rows = pl.ds(r * S, S)
        outb[rows, :] = (resid[rows, :] + reduce_end(r, 1)).astype(BF)

        @pl.when(jnp.logical_not(source))
        def _():
            post(outb.at[rows, :], swapb.at[rows, :], 22 + r, sem_swap.at[1 + r], to_swap)

    def save(r):
        rows = pl.ds(r * S, S)
        live = lax.broadcasted_iota(jnp.int32, (S, FEAT), 0) < lens[r]

        @pl.when(source)
        def _():
            swapb[rows, :] = jnp.where(live, outb[rows, :], jnp.zeros((S, FEAT), BF))

        @pl.when(jnp.logical_not(source))
        def _():
            arrived(swapb.at[rows, :], sem_swap.at[1 + r])
            swapb[rows, :] = jnp.where(live, swapb[rows, :], jnp.zeros((S, FEAT), BF))

        pltpu.make_async_copy(swapb.at[rows, :], y.at[rows, :], loc_sem.at[12 + r]).start()

    def saved(r):
        rows = pl.ds(r * S, S)
        pltpu.make_async_copy(swapb.at[rows, :], y.at[rows, :], loc_sem.at[12 + r]).wait()

    def out(r):
        terms(mixed, go, 0, r, 0)

    def down(r):
        reduce_gone(r, 0)
        terms(hidden, gf, 1024, r, 1)

    def act(step, r):
        step(xm, r * S, S, 1 + r)

    exchanged(gq, 0, 0, WIDE)
    start_q()
    end_swap()
    gather_start(xg, 0, TOK, 0)
    exchanged(go, 1, 0, 512)
    exchanged(gf, 2, 0, 1536)
    early_q(0)
    early_q(1)
    early_q(2)
    early_q(3)
    gather_near(xg, 0, TOK, 0)
    early_q(4)
    early_q(5)
    gather_far(xg, 0, TOK, 0)
    late_q(0)
    gather_core(xg, 0, TOK, 0)
    scales(xg, 0)
    late_q(1)
    scales(xg, S)
    start_o()
    late_q(2)
    last_q(0)
    project(0)
    late_q(3)
    last_q(1)
    project(1)
    last_q(2)
    project(2)
    early_o(0)
    early_o(1)
    early_o(2)
    early_o(3)
    start_g()
    last_q(3)
    project(3)
    early_o(4)
    early_o(5)
    late_o(0)
    retention(0)
    late_o(1)
    late_o(2)
    late_o(3)
    early_g(0)
    early_g(1)
    early_g(2)
    early_g(3)
    start_d()
    retention(1)
    last_o(0)
    last_o(1)
    last_o(2)
    last_o(3)
    early_g(4)
    early_g(5)
    out(0)
    late_g(0)
    late_g(1)
    out(1)
    late_g(2)
    reduce_start(0, 0)
    late_g(3)
    reduce_start(1, 0)
    reduce_relay(0, 0)
    early_d(0)
    early_d(1)
    early_d(2)
    early_d(3)
    reduce_relay(1, 0)
    early_d(4)
    early_d(5)
    add_residual(0)
    act(gather_start, 0)
    late_d(0)
    add_residual(1)
    act(gather_start, 1)
    late_d(1)
    late_d(2)
    act(gather_near, 0)
    late_d(3)
    act(gather_far, 0)
    act(gather_near, 1)
    act(gather_core, 0)
    last_g(0)
    last_g(1)
    last_g(2)
    last_g(3)
    feed(0)
    act(gather_far, 1)
    last_d(0)
    last_d(1)
    last_d(2)
    last_d(3)
    down(0)
    act(gather_core, 1)
    serve_start()
    reduce_start(0, 1)
    feed(1)
    reduce_relay(0, 1)
    down(1)
    serve_end()
    reduce_start(1, 1)
    finish(0)
    reduce_relay(1, 1)
    save(0)
    finish(1)
    save(1)

    for group, (buf, lo, width) in enumerate(((gq, 0, WIDE), (go, 0, 512), (gf, 0, 1536))):
        gone(buf.at[0:112, lo : lo + width], group)
    gather_gone(xg, 0, TOK, 0)
    for r in range(REQS):
        act(gather_gone, r)
        reduce_gone(r, 1)
    left_q()
    left_o()
    left_g()
    left_d()

    @pl.when(source)
    def _():
        for i, srv in enumerate((srvq, srvo, srvf)):
            gone(srv, 11 + i)

    @pl.when(jnp.logical_not(source))
    def _():
        gone(hid, 3)
        for r in range(REQS):
            gone(outb.at[pl.ds(r * S, S), :], 22 + r)

    for one in stores():
        one.wait()
    saved(0)
    saved(1)


def settle(y_in, q_in, f_in, m_in, d_in, y, q, f, m, d, yv, qv, fv, mv, dv, sem):
    sets = ((y_in, yv, y), (q_in, qv, q), (f_in, fv, f), (m_in, mv, m), (d_in, dv, d))
    takes = [pltpu.make_async_copy(a, b, sem.at[i]) for i, (a, b, _) in enumerate(sets)]
    gives = [pltpu.make_async_copy(b, c, sem.at[5 + i]) for i, (_, b, c) in enumerate(sets)]
    for one in takes:
        one.start()
    for one, two in zip(takes, gives):
        one.wait()
        two.start()
    for one in gives:
        one.wait()


def layer(lengths, hidden, qkvg, gateup, out_t, down_t):
    cosine, sine = tables()
    hbm = pl.BlockSpec(memory_space=pl.ANY)
    dma = pltpu.SemaphoreType.DMA
    shapes = (
        jax.ShapeDtypeStruct((TOK, FEAT), BF),
        jax.ShapeDtypeStruct((128, WIDE), BF),
        jax.ShapeDtypeStruct((2, 128, 512), BF),
        jax.ShapeDtypeStruct((512, 128), BF),
        jax.ShapeDtypeStruct((512, 128), BF),
    )
    scratch = [
        pltpu.VMEM((16, HEADS * WIDE), F32),
        pltpu.VMEM((2, 16, FF), F32),
        pltpu.VMEM((16, HEADS * VAL), F32),
        pltpu.VMEM((16, FF), F32),
        pltpu.VMEM((S, KEY // 2), F32),
        pltpu.VMEM((S, KEY // 2), F32),
        pltpu.VMEM((2, 512, 128), BF),
        pltpu.VMEM((8, 16, WIDE), BF),
        pltpu.VMEM((8, 16, 512), BF),
        pltpu.VMEM((8, 16, 1536), BF),
        pltpu.VMEM((128, WIDE), BF),
        pltpu.VMEM((128, 512), BF),
        pltpu.VMEM((128, 1536), BF),
        pltpu.VMEM((TOK, D), BF),
        pltpu.VMEM((TOK, D), BF),
        pltpu.VMEM((D, WIDE), BF),
        pltpu.VMEM((D, 512), BF),
        pltpu.VMEM((D, 1536), BF),
        pltpu.VMEM((TOK, WIDE), F32),
        pltpu.VMEM((TOK, 128), F32),
        pltpu.VMEM((BLOCK, BLOCK), F32),
        pltpu.VMEM((BLOCK, BLOCK), F32),
        pltpu.VMEM((S, KEY), BF),
        pltpu.VMEM((S, KEY), BF),
        pltpu.VMEM((TOK, VAL), BF),
        pltpu.VMEM((TOK, 512), BF),
        pltpu.VMEM((REQS, 8, S, FEAT), BF),
        pltpu.VMEM((2, REQS, 4, S, FEAT), BF),
        pltpu.VMEM((2, REQS, 2, S // 2, FEAT), BF),
        pltpu.VMEM((2, REQS, 2, S, FEAT), BF),
        pltpu.VMEM((TOK, FEAT), F32),
        pltpu.VMEM((TOK, FEAT), BF),
        pltpu.VMEM((TOK, FEAT), BF),
        dma((24,)),
        dma((3,)),
        dma((3,)),
        dma((76,)),
        dma((12,)),
        dma((16,)),
        dma((8,)),
        dma((4,)),
        dma((3,)),
        dma((14,)),
    ]
    results = pl.pallas_call(
        kernel,
        out_shape=shapes,
        in_specs=[pl.BlockSpec(memory_space=pltpu.SMEM)] + [hbm] * 7,
        out_specs=(hbm,) * 5,
        scratch_shapes=scratch,
        compiler_params=pltpu.CompilerParams(
            collective_id=0, has_side_effects=True, vmem_limit_bytes=62 * 1024 * 1024
        ),
    )(lengths, hidden, qkvg, gateup, out_t, down_t, jnp.asarray(cosine), jnp.asarray(sine))
    return pl.pallas_call(
        settle,
        out_shape=shapes,
        in_specs=[hbm] * 5,
        out_specs=(hbm,) * 5,
        scratch_shapes=[pltpu.VMEM(one.shape, one.dtype) for one in shapes] + [dma((10,))],
    )(*results)


def shards(hidden_states, lengths, qkvg_master, gateup_master, out_master, down_master):
    return layer(
        lengths, hidden_states, qkvg_master, gateup_master, out_master.T, down_master.T
    )


def solution(mesh):
    return jax.shard_map(
        shards,
        mesh=mesh,
        in_specs=(
            P("row", "col"),
            P("row"),
            P(("row", "col"), None),
            P(None, ("row", "col"), None),
            P(None, ("row", "col")),
            P(None, ("row", "col")),
        ),
        out_specs=(
            P("row", "col"),
            P("row", "col"),
            P(None, "row", "col"),
            P("col", "row"),
            P("col", "row"),
        ),
        check_vma=False,
    )
```

time: 184 us -> 158 us (0.86)
  Pallas kernels: 177 us -> 157 us
  local copies, waits for them, and re-layouts: 2.97 us -> 0 us
  other arithmetic: 2.9 us -> 0 us
    pallas_call x1 -> x2, Pallas kernels: 177 us -> 157 us  [the longest x1 155 us: layer(): pl.pallas_call(kernel, out_shape=shapes, in_specs=[pl.BlockSpec(memory_sp...]
    unnamed x11 -> x0, local copies, waits for them, and re-layouts: 2.93 us -> none
    select_n x1 -> x0, other arithmetic: 2.1 us -> none  [shards(): output = jnp.where(live.reshape(TOK, 1), y, jnp.zeros_like(y))]
where the time goes in v2:
time: 158 us
  Pallas kernels  157 us (99%)
    pallas_call x1, Pallas kernels, layer(): pl.pallas_call(kernel, out_shape=shapes, in_specs=[pl.BlockSpec(memory_sp...  155 us

profile of v2, /device:TPU:1, one launch (start us, length us, event | category | flops | bytes accessed | tf_op | source)
XLA Modules:
  0.0 157.9 jit_solution(740120690499543419)
XLA Ops:
  0.6 155.0 %shard_map.119 = (bf16[1024,256]{1,0:T(8,128)(2,1)}, bf16[128,1536]{1,0:T(8,128)(2,1)}, bf16[2,128,512]{2,1,0:T(8,128)(2,1)}, bf16[512,128]{1,0:T(8,128)(2,1)}, bf16[512,128]{1,0:T(8,128)(2,1)}) custom-call(s32[2]{0:T(128)} %lens.1, bf16[1024,256]{1,0:T(8,128)(2,1)} %hid.1, f32[16,12288]{1,0:T(8,128)} %qm_hbm.1, f32[2,16,4096]{2,1,0:T(8,128)} %gm_hbm.1, ...), custom_call_target="tpu_custom_call" | custom-call | tf_op jit(solution)/shard_map/pallas_call | solution.py:709
  155.7 2.2 %shard_map.120 = (bf16[1024,256]{1,0:T(8,128)(2,1)}, bf16[128,1536]{1,0:T(8,128)(2,1)}, bf16[2,128,512]{2,1,0:T(8,128)(2,1)}, bf16[512,128]{1,0:T(8,128)(2,1)}, bf16[512,128]{1,0:T(8,128)(2,1)}) custom-call(bf16[1024,256]{1,0:T(8,128)(2,1)} %get-tuple-element.10.y_in, bf16[128,1536]{1,0:T(8,128)(2,1)} %get-tuple-element.11.q_in, ...), custom_call_target="tpu_custom_call" | custom-call | tf_op jit(solution)/shard_map/pallas_call | solution.py:719

commit v3 on v2

--- a/solution.py
+++ b/solution.py
@@ -515,74 +515,74 @@
     gather_near(xg, 0, TOK, 0)
     early_q(4)
     early_q(5)
+    start_o()
+    late_q(0)
     gather_far(xg, 0, TOK, 0)
-    late_q(0)
+    late_q(1)
     gather_core(xg, 0, TOK, 0)
     scales(xg, 0)
-    late_q(1)
+    late_q(2)
     scales(xg, S)
-    start_o()
-    late_q(2)
+    late_q(3)
     last_q(0)
     project(0)
-    late_q(3)
-    last_q(1)
-    project(1)
-    last_q(2)
-    project(2)
     early_o(0)
     early_o(1)
     early_o(2)
     early_o(3)
+    last_q(1)
+    project(1)
+    early_o(4)
+    early_o(5)
+    last_q(2)
+    project(2)
+    late_o(0)
+    late_o(1)
+    late_o(2)
+    late_o(3)
     start_g()
     last_q(3)
     project(3)
-    early_o(4)
-    early_o(5)
-    late_o(0)
     retention(0)
-    late_o(1)
-    late_o(2)
-    late_o(3)
+    last_o(0)
+    last_o(1)
+    last_o(2)
+    last_o(3)
+    out(0)
     early_g(0)
     early_g(1)
     early_g(2)
     early_g(3)
-    start_d()
     retention(1)
-    last_o(0)
-    last_o(1)
-    last_o(2)
-    last_o(3)
+    out(1)
+    reduce_start(0, 0)
     early_g(4)
     early_g(5)
-    out(0)
+    reduce_start(1, 0)
+    reduce_relay(0, 0)
     late_g(0)
     late_g(1)
-    out(1)
     late_g(2)
-    reduce_start(0, 0)
     late_g(3)
-    reduce_start(1, 0)
-    reduce_relay(0, 0)
+    start_d()
+    add_residual(0)
+    act(gather_start, 0)
+    reduce_relay(1, 0)
     early_d(0)
     early_d(1)
     early_d(2)
     early_d(3)
-    reduce_relay(1, 0)
+    add_residual(1)
+    act(gather_start, 1)
+    act(gather_near, 0)
     early_d(4)
     early_d(5)
-    add_residual(0)
-    act(gather_start, 0)
+    act(gather_far, 0)
     late_d(0)
-    add_residual(1)
-    act(gather_start, 1)
     late_d(1)
+    act(gather_near, 1)
     late_d(2)
-    act(gather_near, 0)
     late_d(3)
-    act(gather_far, 0)
-    act(gather_near, 1)
     act(gather_core, 0)
     last_g(0)
     last_g(1)
@@ -590,20 +590,20 @@
     last_g(3)
     feed(0)
     act(gather_far, 1)
+    act(gather_core, 1)
+    feed(1)
     last_d(0)
     last_d(1)
     last_d(2)
     last_d(3)
     down(0)
-    act(gather_core, 1)
+    reduce_start(0, 1)
+    down(1)
     serve_start()
-    reduce_start(0, 1)
-    feed(1)
     reduce_relay(0, 1)
-    down(1)
-    serve_end()
     reduce_start(1, 1)
     finish(0)
+    serve_end()
     reduce_relay(1, 1)
     save(0)
     finish(1)

time: 158 us -> 150 us (0.949)
  Pallas kernels: 157 us -> 150 us
    pallas_call x1, Pallas kernels: 155 us -> 147 us  [layer(): pl.pallas_call(kernel, out_shape=shapes, in_specs=[pl.BlockSpec(memory_sp...]
where the time goes in v3:
time: 150 us
  Pallas kernels  150 us (100%)
    pallas_call x1, Pallas kernels, layer(): pl.pallas_call(kernel, out_shape=shapes, in_specs=[pl.BlockSpec(memory_sp...  147 us

profile of v3, /device:TPU:1, one launch (start us, length us, event | category | flops | bytes accessed | tf_op | source)
XLA Modules:
  0.0 150.2 jit_solution(2313504209617096631)
XLA Ops:
  0.6 147.3 %shard_map.119 = (bf16[1024,256]{1,0:T(8,128)(2,1)}, bf16[128,1536]{1,0:T(8,128)(2,1)}, bf16[2,128,512]{2,1,0:T(8,128)(2,1)}, bf16[512,128]{1,0:T(8,128)(2,1)}, bf16[512,128]{1,0:T(8,128)(2,1)}) custom-call(s32[2]{0:T(128)} %lens.1, bf16[1024,256]{1,0:T(8,128)(2,1)} %hid.1, f32[16,12288]{1,0:T(8,128)} %qm_hbm.1, f32[2,16,4096]{2,1,0:T(8,128)} %gm_hbm.1, ...), custom_call_target="tpu_custom_call" | custom-call | tf_op jit(solution)/shard_map/pallas_call | solution.py:709
  148.0 2.2 %shard_map.120 = (bf16[1024,256]{1,0:T(8,128)(2,1)}, bf16[128,1536]{1,0:T(8,128)(2,1)}, bf16[2,128,512]{2,1,0:T(8,128)(2,1)}, bf16[512,128]{1,0:T(8,128)(2,1)}, bf16[512,128]{1,0:T(8,128)(2,1)}) custom-call(bf16[1024,256]{1,0:T(8,128)(2,1)} %get-tuple-element.10.y_in, bf16[128,1536]{1,0:T(8,128)(2,1)} %get-tuple-element.11.q_in, ...), custom_call_target="tpu_custom_call" | custom-call | tf_op jit(solution)/shard_map/pallas_call | solution.py:719

commit v4 on v2

--- a/solution.py
+++ b/solution.py
@@ -507,105 +507,105 @@
     end_swap()
     gather_start(xg, 0, TOK, 0)
     exchanged(go, 1, 0, 512)
+    start_o()
     exchanged(gf, 2, 0, 1536)
     early_q(0)
     early_q(1)
     early_q(2)
     early_q(3)
+    early_o(0)
+    early_o(1)
+    early_o(2)
+    early_o(3)
     gather_near(xg, 0, TOK, 0)
     early_q(4)
     early_q(5)
+    early_o(4)
+    early_o(5)
+    late_q(0)
+    late_o(0)
     gather_far(xg, 0, TOK, 0)
-    late_q(0)
+    late_q(1)
+    late_o(1)
     gather_core(xg, 0, TOK, 0)
     scales(xg, 0)
-    late_q(1)
+    late_q(2)
+    late_o(2)
     scales(xg, S)
-    start_o()
-    late_q(2)
+    late_q(3)
+    late_o(3)
+    start_g()
     last_q(0)
     project(0)
-    late_q(3)
     last_q(1)
     project(1)
     last_q(2)
     project(2)
-    early_o(0)
-    early_o(1)
-    early_o(2)
-    early_o(3)
-    start_g()
     last_q(3)
     project(3)
-    early_o(4)
-    early_o(5)
-    late_o(0)
-    retention(0)
-    late_o(1)
-    late_o(2)
-    late_o(3)
     early_g(0)
     early_g(1)
-    early_g(2)
-    early_g(3)
-    start_d()
-    retention(1)
+    retention(0)
     last_o(0)
     last_o(1)
     last_o(2)
     last_o(3)
+    out(0)
+    reduce_start(0, 0)
+    early_g(2)
+    early_g(3)
     early_g(4)
     early_g(5)
-    out(0)
+    start_d()
+    retention(1)
     late_g(0)
     late_g(1)
+    reduce_relay(0, 0)
     out(1)
+    reduce_start(1, 0)
     late_g(2)
-    reduce_start(0, 0)
     late_g(3)
-    reduce_start(1, 0)
-    reduce_relay(0, 0)
     early_d(0)
     early_d(1)
     early_d(2)
     early_d(3)
+    add_residual(0)
+    act(gather_start, 0)
     reduce_relay(1, 0)
     early_d(4)
     early_d(5)
-    add_residual(0)
-    act(gather_start, 0)
-    late_d(0)
+    act(gather_near, 0)
     add_residual(1)
     act(gather_start, 1)
+    late_d(0)
     late_d(1)
-    late_d(2)
-    act(gather_near, 0)
-    late_d(3)
     act(gather_far, 0)
     act(gather_near, 1)
+    late_d(2)
+    late_d(3)
     act(gather_core, 0)
     last_g(0)
     last_g(1)
     last_g(2)
     last_g(3)
     feed(0)
-    act(gather_far, 1)
     last_d(0)
     last_d(1)
     last_d(2)
     last_d(3)
     down(0)
+    reduce_start(0, 1)
+    act(gather_far, 1)
     act(gather_core, 1)
-    serve_start()
-    reduce_start(0, 1)
     feed(1)
     reduce_relay(0, 1)
     down(1)
-    serve_end()
     reduce_start(1, 1)
     finish(0)
+    serve_start()
     reduce_relay(1, 1)
     save(0)
+    serve_end()
     finish(1)
     save(1)
 

time: 158 us -> 142 us (0.90)
  Pallas kernels: 157 us -> 141 us
    pallas_call x1, Pallas kernels: 155 us -> 138 us  [layer(): pl.pallas_call(kernel, out_shape=shapes, in_specs=[pl.BlockSpec(memory_sp...]
where the time goes in v4:
time: 142 us; the launch traced here: 141 us
  Pallas kernels  141 us (99%)
    pallas_call x1, Pallas kernels, layer(): pl.pallas_call(kernel, out_shape=shapes, in_specs=[pl.BlockSpec(memory_sp...  138 us

profile of v4, /device:TPU:1, one launch (start us, length us, event | category | flops | bytes accessed | tf_op | source)
XLA Modules:
  0.0 141.3 jit_solution(4011475885568922841)
XLA Ops:
  0.6 138.5 %shard_map.119 = (bf16[1024,256]{1,0:T(8,128)(2,1)}, bf16[128,1536]{1,0:T(8,128)(2,1)}, bf16[2,128,512]{2,1,0:T(8,128)(2,1)}, bf16[512,128]{1,0:T(8,128)(2,1)}, bf16[512,128]{1,0:T(8,128)(2,1)}) custom-call(s32[2]{0:T(128)} %lens.1, bf16[1024,256]{1,0:T(8,128)(2,1)} %hid.1, f32[16,12288]{1,0:T(8,128)} %qm_hbm.1, f32[2,16,4096]{2,1,0:T(8,128)} %gm_hbm.1, ...), custom_call_target="tpu_custom_call" | custom-call | tf_op jit(solution)/shard_map/pallas_call | solution.py:709
  139.1 2.2 %shard_map.120 = (bf16[1024,256]{1,0:T(8,128)(2,1)}, bf16[128,1536]{1,0:T(8,128)(2,1)}, bf16[2,128,512]{2,1,0:T(8,128)(2,1)}, bf16[512,128]{1,0:T(8,128)(2,1)}, bf16[512,128]{1,0:T(8,128)(2,1)}) custom-call(bf16[1024,256]{1,0:T(8,128)(2,1)} %get-tuple-element.10.y_in, bf16[128,1536]{1,0:T(8,128)(2,1)} %get-tuple-element.11.q_in, ...), custom_call_target="tpu_custom_call" | custom-call | tf_op jit(solution)/shard_map/pallas_call | solution.py:719

commit v5 on v4

--- a/solution.py
+++ b/solution.py
@@ -166,21 +166,7 @@
         one.wait()
     for i in range(8):
         sbo[i] = om[:, i * VAL : (i + 1) * VAL].astype(BF)
-        sbf[i, :, 0:512] = gm[0, :, i * 512 : (i + 1) * 512].astype(BF)
-        sbf[i, :, 512:1024] = gm[1, :, i * 512 : (i + 1) * 512].astype(BF)
-        sbf[i, :, 1024:1536] = dm[:, i * 512 : (i + 1) * 512].astype(BF)
     exchange(sbo, go, 1, 0, 512)
-    exchange(sbf, gf, 2, 0, 1536)
-
-    head = c * 4 + z
-    rate = jnp.float32(0.0)
-    for i in range(HEADS):
-        rate = jnp.where(head == i, jnp.float32(math.log1p(-(2.0 ** (-5 - i)))), rate)
-    lag = lax.broadcasted_iota(jnp.int32, (BLOCK, BLOCK), 0) - lax.broadcasted_iota(
-        jnp.int32, (BLOCK, BLOCK), 1
-    )
-    near[...] = jnp.where(lag >= 0, jnp.exp(jnp.maximum(lag, 0).astype(F32) * rate), 0.0)
-    far[...] = jnp.exp((lag + BLOCK).astype(F32) * rate)
 
     def act_ref(buf, rows, slot):
         return buf.at[rows, lanes(slot)]
@@ -502,13 +488,32 @@
     def act(step, r):
         step(xm, r * S, S, 1 + r)
 
+    def deal_feed():
+        for i in range(8):
+            sbf[i, :, 0:512] = gm[0, :, i * 512 : (i + 1) * 512].astype(BF)
+            sbf[i, :, 512:1024] = gm[1, :, i * 512 : (i + 1) * 512].astype(BF)
+            sbf[i, :, 1024:1536] = dm[:, i * 512 : (i + 1) * 512].astype(BF)
+        exchange(sbf, gf, 2, 0, 1536)
+
+    def decays():
+        head = c * 4 + z
+        rate = jnp.float32(0.0)
+        for i in range(HEADS):
+            rate = jnp.where(head == i, jnp.float32(math.log1p(-(2.0 ** (-5 - i)))), rate)
+        lag = lax.broadcasted_iota(jnp.int32, (BLOCK, BLOCK), 0) - lax.broadcasted_iota(
+            jnp.int32, (BLOCK, BLOCK), 1
+        )
+        near[...] = jnp.where(lag >= 0, jnp.exp(jnp.maximum(lag, 0).astype(F32) * rate), 0.0)
+        far[...] = jnp.exp((lag + BLOCK).astype(F32) * rate)
+
     exchanged(gq, 0, 0, WIDE)
     start_q()
+    deal_feed()
+    decays()
     end_swap()
     gather_start(xg, 0, TOK, 0)
     exchanged(go, 1, 0, 512)
     start_o()
-    exchanged(gf, 2, 0, 1536)
     early_q(0)
     early_q(1)
     early_q(2)
@@ -522,6 +527,7 @@
     early_q(5)
     early_o(4)
     early_o(5)
+    exchanged(gf, 2, 0, 1536)
     late_q(0)
     late_o(0)
     gather_far(xg, 0, TOK, 0)

time: 142 us -> 142 us (level)
  no operation moved by 1% of the time
where the time goes in v5:
time: 142 us; the launch traced here: 141 us
  Pallas kernels  141 us (99%)
    pallas_call x1, Pallas kernels, layer(): pl.pallas_call(kernel, out_shape=shapes, in_specs=[pl.BlockSpec(memory_sp...  139 us

profile of v5, /device:TPU:1, one launch (start us, length us, event | category | flops | bytes accessed | tf_op | source)
XLA Modules:
  0.0 141.4 jit_solution(4924455317753654378)
XLA Ops:
  0.6 138.5 %shard_map.119 = (bf16[1024,256]{1,0:T(8,128)(2,1)}, bf16[128,1536]{1,0:T(8,128)(2,1)}, bf16[2,128,512]{2,1,0:T(8,128)(2,1)}, bf16[512,128]{1,0:T(8,128)(2,1)}, bf16[512,128]{1,0:T(8,128)(2,1)}) custom-call(s32[2]{0:T(128)} %lens.1, bf16[1024,256]{1,0:T(8,128)(2,1)} %hid.1, f32[16,12288]{1,0:T(8,128)} %qm_hbm.1, f32[2,16,4096]{2,1,0:T(8,128)} %gm_hbm.1, ...), custom_call_target="tpu_custom_call" | custom-call | tf_op jit(solution)/shard_map/pallas_call | solution.py:715
  139.2 2.2 %shard_map.120 = (bf16[1024,256]{1,0:T(8,128)(2,1)}, bf16[128,1536]{1,0:T(8,128)(2,1)}, bf16[2,128,512]{2,1,0:T(8,128)(2,1)}, bf16[512,128]{1,0:T(8,128)(2,1)}, bf16[512,128]{1,0:T(8,128)(2,1)}) custom-call(bf16[1024,256]{1,0:T(8,128)(2,1)} %get-tuple-element.10.y_in, bf16[128,1536]{1,0:T(8,128)(2,1)} %get-tuple-element.11.q_in, ...), custom_call_target="tpu_custom_call" | custom-call | tf_op jit(solution)/shard_map/pallas_call | solution.py:725
